TPU v7x, 32 devices: a whole 2x2x4 slice. The times are simulated.
32 devices in a mesh: seq: 8 (over z, y), mp: 4 (over x, core).
Axes of the slice: x: 2, y: 2, z: 4, core: 2. Of those that a mesh axis runs over, the one named last changes fastest.
Arguments:
- block_input: bfloat16 [1, 1280, 2560], P(None, 'seq'), may hold values from -6 to 6
- mix_gain: float32 [2560], replicated, may hold values from 0.5 to 1.5
- x_weight: bfloat16 [2560, 2560], P(None, 'mp'), may hold values from -0.125 to 0.125
- y_weight: bfloat16 [2560, 2560], P(None, 'mp'), may hold values from -0.125 to 0.125
- conv_weight: float32 [4, 2560], P(None, 'mp'), may hold values from -3 to 3
- conv_bias: float32 [2560], P('mp'), may hold values from -3 to 3
- input_gate: bfloat16 [256, 2560], P(None, 'mp'), may hold values from -0.375 to 0.375
- decay_gate: bfloat16 [256, 2560], P(None, 'mp'), may hold values from -0.375 to 0.375
- decay_param: float32 [2560], P('mp'), may hold values from -13 to -5
- out_weight: bfloat16 [2560, 2560], P('mp'), may hold values from -0.125 to 0.125
- ffn_gain: float32 [2560], replicated, may hold values from 0.5 to 1.5
- gate_weight: bfloat16 [2560, 7680], P(None, 'mp'), may hold values from -0.125 to 0.125
- up_weight: bfloat16 [2560, 7680], P(None, 'mp'), may hold values from -0.125 to 0.125
- down_weight: bfloat16 [7680, 2560], P('mp'), may hold values from -0.0625 to 0.0625
- out_cotangent: bfloat16 [1, 1280, 2560], P(None, 'seq'), may hold values from -6 to 6
Outputs:
- block_output: bfloat16 [1, 1280, 2560], P(None, 'seq')
- input_grad: bfloat16 [1, 1280, 2560], P(None, 'seq')
- mix_gain_grad: float32 [2560], P('seq')
- x_weight_grad: float32 [2560, 2560], P('seq', 'mp')
- y_weight_grad: float32 [2560, 2560], P('seq', 'mp')
- conv_weight_grad: float32 [4, 2560], P(None, ('mp', 'seq'))
- conv_bias_grad: float32 [2560], P(('mp', 'seq'))
- input_gate_grad: float32 [256, 2560], P('seq', 'mp')
- decay_gate_grad: float32 [256, 2560], P('seq', 'mp')
- decay_param_grad: float32 [2560], P(('mp', 'seq'))
- out_weight_grad: float32 [2560, 2560], P('mp', 'seq')
- ffn_gain_grad: float32 [2560], P('seq')
- gate_weight_grad: float32 [2560, 7680], P('seq', 'mp')
- up_weight_grad: float32 [2560, 7680], P('seq', 'mp')
- down_weight_grad: float32 [7680, 2560], P('mp', 'seq')
All inputs are finite; a program needn't handle non-finite values.
Results may differ from a plain program's by a relative error of at most 0.009.
Values may be sent and summed in bfloat16 or wider, within the bound.
No kernel may reach another device: no remote copies, remote signals or barrier semaphores. Data moves between devices by JAX's collectives and lax.ppermute only.
A program may use at most 320 MiB of HBM per device.

v0:
```python
import jax
import jax.numpy as jnp
from jax import lax
from jax.sharding import PartitionSpec as P

EPS = 1e-06


def passed_along(shard, axis, by):
    size = lax.axis_size(axis)
    pairs = [(i, i + by) for i in range(size) if 0 <= i + by < size]
    return lax.ppermute(shard, axis, pairs)


def carried_in(value, axis, join, neutral, backward):
    count, mine = (lax.axis_size(axis), lax.axis_index(axis))
    pieces = jax.tree.map(lambda part: lax.all_gather(part, axis), value)
    if backward:
        pieces = jax.tree.map(lambda part: part[::-1], pieces)
        mine = count - 1 - mine
    so_far = jax.tree.map(
        lambda part, zero: jnp.full_like(part, 0) + jnp.asarray(zero, part.dtype), value, neutral
    )

    def lap(position, so_far):
        longer = join(so_far, jax.tree.map(lambda part: part[position], pieces))
        return jax.tree.map(lambda new, old: jnp.where(position < mine, new, old), longer, so_far)

    return lax.fori_loop(0, count - 1, lap, so_far)


def gelu_tanh(values):
    return jax.nn.gelu(values, approximate=True)


def gelu_slope(values):
    _, pullback = jax.vjp(gelu_tanh, values)
    return pullback(jnp.ones_like(values))[0]


def bdot(left, right):
    return jnp.dot(left, right, preferred_element_type=jnp.float32)


def link_pairs(earlier, later):
    return (earlier[0] * later[0], later[0] * earlier[1] + later[1])


def per_device(
    block_input,
    mix_gain,
    x_weight,
    y_weight,
    conv_weight,
    conv_bias,
    input_gate,
    decay_gate,
    decay_param,
    out_weight,
    ffn_gain,
    gate_weight,
    up_weight,
    down_weight,
    out_cotangent,
):
    seq_count, group_len, model_width = block_input.shape
    local_w = x_weight.shape[1]
    head_size = input_gate.shape[0]
    full_w = local_w * lax.axis_size("mp")
    row_count = seq_count * group_len
    owner = lax.axis_index("mp")
    row_heads = jnp.arange(full_w, dtype=jnp.int32) // head_size
    col_heads = (owner * local_w + jnp.arange(local_w, dtype=jnp.int32)) // head_size
    head_mask = row_heads[:, None] == col_heads[None, :]
    dense_x = jnp.where(
        head_mask, jnp.tile(input_gate, (full_w // head_size, 1)), jnp.zeros((), jnp.bfloat16)
    )
    dense_a = jnp.where(
        head_mask, jnp.tile(decay_gate, (full_w // head_size, 1)), jnp.zeros((), jnp.bfloat16)
    )
    inp = block_input.reshape(row_count, model_width).astype(jnp.float32)
    r_one = lax.rsqrt(jnp.mean(inp * inp, axis=-1, keepdims=True) + EPS)
    n_one = inp * r_one
    normed1 = (n_one * mix_gain).astype(jnp.bfloat16)
    x_branch = bdot(normed1, x_weight)
    y_branch = bdot(normed1, y_weight)
    y_gated = gelu_tanh(y_branch)
    x_three = x_branch.reshape(seq_count, group_len, local_w)
    before = passed_along(x_three[:, group_len - 3 :, :], "seq", 1)
    padded = jnp.concatenate([before, x_three], axis=1)
    conv_three = conv_bias + sum(
        (conv_weight[offset] * padded[:, offset : offset + group_len] for offset in range(4))
    )
    conv_out = conv_three.reshape(row_count, local_w)
    conv_low = conv_out.astype(jnp.bfloat16)
    gathered = lax.all_gather(conv_low, "mp", axis=1, tiled=True)
    gate_x = jax.nn.sigmoid(bdot(gathered, dense_x))
    gate_a = jax.nn.sigmoid(bdot(gathered, dense_a))
    softer = jax.nn.softplus(decay_param)
    log_decay = -8.0 * softer * gate_a
    decay = jnp.exp(log_decay)
    mult = jnp.sqrt(-jnp.expm1(2.0 * log_decay))
    drive = conv_out * gate_x * mult
    decay_three = decay.reshape(seq_count, group_len, local_w)
    prod_three, local_state = lax.associative_scan(
        link_pairs, (decay_three, drive.reshape(seq_count, group_len, local_w)), axis=1
    )
    block_prod = prod_three[:, -1]
    ones_init = jnp.ones((seq_count, local_w), jnp.float32)
    zero_init = jnp.zeros((seq_count, local_w), jnp.float32)
    carried = carried_in(
        (block_prod, local_state[:, -1]), "seq", link_pairs, (ones_init, zero_init), False
    )
    state_in = carried[1]
    hidden_three = local_state + prod_three * state_in[:, None, :]
    hidden = hidden_three.reshape(row_count, local_w)
    mixed = (hidden * y_gated).astype(jnp.bfloat16)
    x_one = inp + lax.psum(bdot(mixed, out_weight), "mp")
    r_two = lax.rsqrt(jnp.mean(x_one * x_one, axis=-1, keepdims=True) + EPS)
    n_two = x_one * r_two
    normed2 = (n_two * ffn_gain).astype(jnp.bfloat16)
    gate_pre = bdot(normed2, gate_weight)
    up_pre = bdot(normed2, up_weight)
    act = (gelu_tanh(gate_pre) * up_pre).astype(jnp.bfloat16)
    ffn_out = lax.psum(bdot(act, down_weight), "mp")
    block_output = (x_one + ffn_out).astype(jnp.bfloat16).reshape(seq_count, group_len, model_width)
    cot_low = out_cotangent.reshape(row_count, model_width)
    cot = cot_low.astype(jnp.float32)
    d_act = bdot(cot_low, down_weight.T)
    g_down = bdot(act.T, cot_low)
    d_gate = (d_act * up_pre * gelu_slope(gate_pre)).astype(jnp.bfloat16)
    d_up = (d_act * gelu_tanh(gate_pre)).astype(jnp.bfloat16)
    g_gate = bdot(normed2.T, d_gate)
    g_up = bdot(normed2.T, d_up)
    d_n_two = lax.psum(bdot(d_gate, gate_weight.T) + bdot(d_up, up_weight.T), "mp")
    g_ffn_gain = jnp.sum(d_n_two * n_two, axis=0)
    e_two = ffn_gain * d_n_two
    d_x_one = cot + r_two * (e_two - n_two * jnp.mean(e_two * n_two, axis=-1, keepdims=True))
    d_x_low = d_x_one.astype(jnp.bfloat16)
    g_out = bdot(mixed.T, d_x_low)
    d_mixed = bdot(d_x_low, out_weight.T)
    d_y_low = (d_mixed * hidden * gelu_slope(y_branch)).astype(jnp.bfloat16)
    direct = (d_mixed * y_gated).reshape(seq_count, group_len, local_w)
    decay_next = jnp.concatenate(
        [decay_three[:, 1:], jnp.ones((seq_count, 1, local_w), jnp.float32)], axis=1
    )
    after_prod, local_lam = lax.associative_scan(
        link_pairs, (decay_next, direct), reverse=True, axis=1
    )
    first_term = decay_three[:, 0] * local_lam[:, 0]
    returned = carried_in((block_prod, first_term), "seq", link_pairs, (ones_init, zero_init), True)
    lam = (local_lam + after_prod * returned[1][:, None, :]).reshape(row_count, local_w)
    hidden_prev = jnp.concatenate([state_in[:, None, :], hidden_three[:, :-1]], axis=1).reshape(
        row_count, local_w
    )
    d_log = lam * hidden_prev * decay - lam * conv_out * gate_x * decay * decay / mult
    g_decay = jnp.sum(d_log * (-8.0 * gate_a) * jax.nn.sigmoid(decay_param), axis=0)
    d_gx = (lam * conv_out * mult * gate_x * (1.0 - gate_x)).astype(jnp.bfloat16)
    d_ga = (d_log * (-8.0 * softer) * gate_a * (1.0 - gate_a)).astype(jnp.bfloat16)
    dense_gx = jnp.where(head_mask, bdot(gathered.T, d_gx), 0.0)
    dense_ga = jnp.where(head_mask, bdot(gathered.T, d_ga), 0.0)
    g_input_gate = jnp.sum(dense_gx.reshape(full_w // head_size, head_size, local_w), axis=0)
    g_decay_gate = jnp.sum(dense_ga.reshape(full_w // head_size, head_size, local_w), axis=0)
    back_terms = bdot(d_gx, dense_x.T) + bdot(d_ga, dense_a.T)
    back_own = lax.psum_scatter(back_terms, "mp", scatter_dimension=1, tiled=True)
    d_conv = lam * gate_x * mult + back_own
    g_conv_bias = jnp.sum(d_conv, axis=0)
    d_conv_three = d_conv.reshape(seq_count, group_len, local_w)
    g_conv = jnp.stack(
        [
            jnp.sum(d_conv_three * padded[:, offset : offset + group_len], axis=(0, 1))
            for offset in range(4)
        ]
    )
    later_rows = passed_along(d_conv_three[:, :3, :], "seq", -1)
    padded_back = jnp.concatenate([d_conv_three, later_rows], axis=1)
    d_x_three = sum(
        (
            conv_weight[offset] * padded_back[:, 3 - offset : 3 - offset + group_len]
            for offset in range(4)
        )
    )
    d_x_branch = d_x_three.reshape(row_count, local_w).astype(jnp.bfloat16)
    g_x = bdot(normed1.T, d_x_branch)
    g_y = bdot(normed1.T, d_y_low)
    d_n_one = lax.psum(bdot(d_x_branch, x_weight.T) + bdot(d_y_low, y_weight.T), "mp")
    g_mix_gain = jnp.sum(d_n_one * n_one, axis=0)
    e_one = mix_gain * d_n_one
    d_input = d_x_one + r_one * (e_one - n_one * jnp.mean(e_one * n_one, axis=-1, keepdims=True))
    input_grad = d_input.astype(jnp.bfloat16).reshape(seq_count, group_len, model_width)
    summed = (
        lax.psum_scatter(g_mix_gain, "seq", scatter_dimension=0, tiled=True),
        lax.psum_scatter(g_x, "seq", scatter_dimension=0, tiled=True),
        lax.psum_scatter(g_y, "seq", scatter_dimension=0, tiled=True),
        lax.psum_scatter(g_conv, "seq", scatter_dimension=1, tiled=True),
        lax.psum_scatter(g_conv_bias, "seq", scatter_dimension=0, tiled=True),
        lax.psum_scatter(g_input_gate, "seq", scatter_dimension=0, tiled=True),
        lax.psum_scatter(g_decay_gate, "seq", scatter_dimension=0, tiled=True),
        lax.psum_scatter(g_decay, "seq", scatter_dimension=0, tiled=True),
        lax.psum_scatter(g_out, "seq", scatter_dimension=1, tiled=True),
        lax.psum_scatter(g_ffn_gain, "seq", scatter_dimension=0, tiled=True),
        lax.psum_scatter(g_gate, "seq", scatter_dimension=0, tiled=True),
        lax.psum_scatter(g_up, "seq", scatter_dimension=0, tiled=True),
        lax.psum_scatter(g_down, "seq", scatter_dimension=1, tiled=True),
    )
    return (
        block_output,
        input_grad,
        summed[0],
        summed[1],
        summed[2],
        summed[3],
        summed[4],
        summed[5],
        summed[6],
        summed[7],
        summed[8],
        summed[9],
        summed[10],
        summed[11],
        summed[12],
    )


def solution(mesh):
    in_specs = (
        P(None, "seq", None),
        P(),
        P(None, "mp"),
        P(None, "mp"),
        P(None, "mp"),
        P("mp"),
        P(None, "mp"),
        P(None, "mp"),
        P("mp"),
        P("mp", None),
        P(),
        P(None, "mp"),
        P(None, "mp"),
        P("mp", None),
        P(None, "seq", None),
    )
    out_specs = (
        P(None, "seq", None),
        P(None, "seq", None),
        P("seq"),
        P("seq", "mp"),
        P("seq", "mp"),
        P(None, ("mp", "seq")),
        P(("mp", "seq")),
        P("seq", "mp"),
        P("seq", "mp"),
        P(("mp", "seq")),
        P("mp", "seq"),
        P("seq"),
        P("seq", "mp"),
        P("seq", "mp"),
        P("mp", "seq"),
    )
    return jax.shard_map(
        per_device, mesh=mesh, in_specs=in_specs, out_specs=out_specs, check_vma=False
    )
```

profile of v0, /device:TPU:0, one launch (start us, length us, event | category | flops | bytes accessed | tf_op | source)
XLA Modules:
  0.0 2169.0 jit_solution(16874175498636065759)
XLA Ops:
  8.8 3.1 fusion.102
  12.7 4.9 collective-permute-start
  21.0 8.8 all_gather.14
  111.2 30.8 %all_gather.15 = f32[8,1,640]{2,1,0:T(1,128)S(1)} all-gather(f32[1,1,640]{2,1,0:T(1,128)S(1)} %slice_add_fusion.2), channel_id=1, replica_groups=mesh['seq'=8,'mp'=4] {'seq'}, dimensions={0}, use_global_device_ids=true | all-gather | bytes 23040 | tf_op jit(solution)/shard_map/all_gather | solution.py:17
  145.3 30.4 %all_gather.16 = f32[8,1,640]{2,1,0:T(1,128)S(1)} all-gather(f32[1,1,640]{2,1,0:T(1,128)S(1)} %slice_add_fusion.1), channel_id=1, replica_groups=mesh['seq'=8,'mp'=4] {'seq'}, dimensions={0}, use_global_device_ids=true | all-gather | bytes 23040 | tf_op jit(solution)/shard_map/all_gather | solution.py:17
  176.1 3.6 fusion.67
  181.9 42.5 %all-reduce.68.cloned.1.call-done = f32[160,2560]{1,0:T(8,128)} async-done(((f32[160,2560]{1,0:T(8,128)}), f32[160,2560]{1,0:T(8,128)}) %all-reduce.68.cloned.1.call-update) | async-done | bytes 1638416 | tf_op jit(solution)/shard_map/psum | solution.py:118
  227.8 6.2 fusion.118
  236.5 8.1 multiply_convert_fusion.1
  244.5 3.3 fusion.120
  247.9 8.3 convolution_add_fusion.2
  264.0 3.0 slice.534
  267.1 3.1 slice.527
  270.1 3.0 slice.529
  273.1 27.2 %all-reduce.70.cloned.1.call-done = f32[160,2560]{1,0:T(8,128)} async-done(((f32[160,2560]{1,0:T(8,128)}), f32[160,2560]{1,0:T(8,128)}) %all-reduce.70.cloned.1.call-update) | async-done | bytes 1638416 | tf_op jit(solution)/shard_map/psum | solution.py:135
  300.4 3.2 multiply_reduce_fusion
  308.1 5.6 reverse.8
  433.8 2.5 pad.215
  440.6 5.6 rev.17
  446.2 30.5 %all_gather.17 = f32[8,1,640]{2,1,0:T(1,128)S(1)} all-gather(f32[1,1,640]{2,1,0:T(1,128)S(1)} %add_multiply_fusion.20), channel_id=1, replica_groups=mesh['seq'=8,'mp'=4] {'seq'}, dimensions={0}, use_global_device_ids=true | all-gather | bytes 23040 | tf_op jit(solution)/shard_map/all_gather | solution.py:17
  476.7 4.8 while.29
  484.0 2.5 pad.229
  488.4 5.6 rev.18
  502.8 7.1 fusion.119
  509.8 21.3 reduce-scatter.13.cloned.1.call-done
  537.1 3.5 collective-permute-done.1
  542.5 3.3 fusion.78
  549.5 3.6 compare_select_fusion
  553.0 4.2 reduce_sum.137
  557.3 3.6 compare_select_fusion.1
  560.9 4.2 reduce_sum.136
  565.2 4.0 fusion.71
  570.3 4.0 fusion.98
  575.3 4.1 fusion.33
  580.7 8.4 fusion.36
  590.4 8.2 fusion.123
  599.7 8.4 fusion.122
  612.1 60.4 %all-reduce.72.cloned.1.call-done = (f32[160,2560]{1,0:T(8,128)}, f32[160,2560]{1,0:T(8,128)}) async-done(((f32[160,2560]{1,0:T(8,128)}, f32[160,2560]{1,0:T(8,128)}), (f32[160,2560]{1,0:T(8,128)}, f32[160,2560]{1,0:T(8,128)})) %all-reduce.72.cloned.1.call-update) | async-done | bytes 3276816 | tf_op jit(solution)/shard_map/psum | solution.py:125
  674.5 37.3 %all-reduce.62 = (f32[2560]{0:T(1024)S(1)}, f32[640]{0:T(1024)S(1)}, f32[640]{0:T(1024)S(1)}, f32[2560]{0:T(1024)S(1)}) all-reduce(f32[2560]{0:T(1024)S(1)} %get-tuple-element.243, f32[640]{0:T(1024)S(1)} %get-tuple-element.248, f32[640]{0:T(1024)S(1)} %get-tuple-element.281, ...), channel_id=3, replica_groups=mesh['seq'=8,'mp'=4] {'seq'}, use_global_device_ids=true, to_apply=%region_14.15.clone | all-reduce | flops 6400 | bytes 51200
  714.3 3.1 fusion.31
  718.9 20.2 reduce-scatter.21.cloned.1.call-done
  739.1 65.6 %reduce-scatter.19.cloned.1.call-done = f32[32,640]{1,0:T(8,128)} async-done(((f32[256,640]{1,0:T(8,128)}), f32[32,640]{1,0:T(8,128)}) %reduce-scatter.19.cloned.1.call-update) | async-done | bytes 81936 | tf_op jit(solution)/shard_map/reduce_scatter | solution.py:197
  804.7 125.0 %reduce-scatter.23.cloned.1.call-done = f32[640,320]{0,1:T(8,128)} async-done(((f32[640,2560]{0,1:T(8,128)}), f32[640,320]{0,1:T(8,128)}) %reduce-scatter.23.cloned.1.call-update) | async-done | bytes 819216 | tf_op jit(solution)/shard_map/reduce_scatter | solution.py:200
  929.8 125.2 %reduce-scatter.17.cloned.1.call-done = f32[320,640]{1,0:T(8,128)} async-done(((f32[2560,640]{1,0:T(8,128)}), f32[320,640]{1,0:T(8,128)}) %reduce-scatter.17.cloned.1.call-update) | async-done | bytes 819216 | tf_op jit(solution)/shard_map/reduce_scatter | solution.py:194
  1055.0 125.1 %reduce-scatter.15.cloned.1.call-done = f32[320,640]{1,0:T(8,128)} async-done(((f32[2560,640]{1,0:T(8,128)}), f32[320,640]{1,0:T(8,128)}) %reduce-scatter.15.cloned.1.call-update) | async-done | bytes 819216 | tf_op jit(solution)/shard_map/reduce_scatter | solution.py:193
  1180.1 327.6 %reduce-scatter.29.cloned.1.call-done = f32[1920,320]{0,1:T(8,128)} async-done(((f32[1920,2560]{0,1:T(8,128)}), f32[1920,320]{0,1:T(8,128)}) %reduce-scatter.29.cloned.1.call-update) | async-done | bytes 2457616 | tf_op jit(solution)/shard_map/reduce_scatter | solution.py:204
  1507.6 327.2 %reduce-scatter.27.cloned.1.call-done = f32[320,1920]{1,0:T(8,128)} async-done(((f32[2560,1920]{1,0:T(8,128)}), f32[320,1920]{1,0:T(8,128)}) %reduce-scatter.27.cloned.1.call-update) | async-done | bytes 2457616 | tf_op jit(solution)/shard_map/reduce_scatter | solution.py:203
  1834.8 327.2 %reduce-scatter.25.cloned.1.call-done = f32[320,1920]{1,0:T(8,128)} async-done(((f32[2560,1920]{1,0:T(8,128)}), f32[320,1920]{1,0:T(8,128)}) %reduce-scatter.25.cloned.1.call-update) | async-done | bytes 2457616 | tf_op jit(solution)/shard_map/reduce_scatter | solution.py:202
  (486 shorter events, 278.8 us)
Async XLA Ops:
  7.2 168.8 %copy-start = (bf16[2560,640]{1,0:T(8,128)(2,1)S(1)}, bf16[2560,640]{1,0:T(8,128)(2,1)}, u32[]{:S(2)}) copy-start(bf16[2560,640]{1,0:T(8,128)(2,1)} %param.22) | copy-start | bytes 9830404
  7.2 217.2 %all-reduce.68.cloned.1.call-start = ((), (), s32[]{:S(2)}) async-start(), calls=%async_computation.10 | async-start | bytes 3276800 | tf_op jit(solution)/shard_map/psum | solution.py:118
  8.8 167.2 %copy-start.59 = (f32[160]{0:T(256)}, f32[160]{0:T(256)S(1)}, u32[]{:S(2)}) copy-start(f32[160]{0:T(256)S(1)} %add_rsqrt_fusion.1) | copy-start | bytes 1924
  8.8 8.8 copy-start.82
  8.8 9.4 copy-start.79
  12.7 8.1 collective-permute-start
  18.2 13.4 copy-start.56
  20.7 9.9 copy-start.13
  20.7 10.0 copy-start.11
  20.8 9.9 copy-start.64
  21.0 10.5 copy-start.21
  100.1 8.8 copy-start.77
  106.9 69.2 %copy-start.50 = (f32[2560]{0:T(1024)S(1)}, f32[2560]{0:T(1024)}, u32[]{:S(2)}) copy-start(f32[2560]{0:T(1024)} %param.20) | copy-start | bytes 30724
  176.0 3.6 copy-start.53
  181.6 45.9 %copy-start.55 = (f32[2560]{0:T(1024)S(1)}, f32[2560]{0:T(1024)}, u32[]{:S(2)}) copy-start(f32[2560]{0:T(1024)} %param.29) | copy-start | bytes 30724
  181.7 118.7 %all-reduce.70.cloned.1.call-start = ((), (), s32[]{:S(2)}) async-start(), calls=%async_computation.11 | async-start | bytes 3276800 | tf_op jit(solution)/shard_map/psum | solution.py:135
  227.6 6.4 slice-start
  227.8 6.2 copy-start.6
  227.8 6.3 slice-start.1
  227.8 6.7 slice-start.2
  256.2 274.9 %reduce-scatter.13.cloned.1.call-start = ((), (), s32[]{:S(2)}) async-start(), calls=%async_computation.12 | async-start | bytes 2048000 | tf_op jit(solution)/shard_map/reduce_scatter | solution.py:165
  407.9 8.6 copy-start.80
  422.7 7.9 copy-start.78
  433.8 42.9 %copy-start.58 = (f32[1,640]{1,0:T(1,128)S(1)}, f32[1,640]{1,0:T(1,128)}, u32[]{:S(2)}) copy-start(f32[1,640]{1,0:T(1,128)} %custom-call.1) | copy-start | bytes 7684
  481.5 12.6 copy-start.54
  481.5 12.6 copy-start.57
  481.5 12.6 copy-start.76
  494.1 4.1 copy-start.14
  502.7 108.0 %reduce-scatter.31.cloned.1.call-start = ((), (), s32[]{:S(2)}) async-start(), calls=%async_computation.21 | async-start | bytes 368640
  502.8 28.4 %copy-start.65 = (f32[1,3,640]{2,1,0:T(4,128)S(1)}, f32[1,3,640]{2,1,0:T(4,128)}, u32[]{:S(2)}) copy-start(f32[1,3,640]{2,1,0:T(4,128)} %copy-done.64) | copy-start | bytes 23044
  509.8 30.8 %copy-start.67 = (f32[640]{0:T(1024)S(1)}, f32[640]{0:T(1024)}, u32[]{:S(2)}) copy-start(f32[640]{0:T(1024)} %copy-done.66) | copy-start | bytes 7684
  509.8 30.8 %copy-start.69 = (f32[640]{0:T(1024)S(1)}, f32[640]{0:T(1024)}, u32[]{:S(2)}) copy-start(f32[640]{0:T(1024)} %copy-done.68) | copy-start | bytes 7684
  509.8 30.8 %copy-start.71 = (f32[640]{0:T(1024)S(1)}, f32[640]{0:T(1024)}, u32[]{:S(2)}) copy-start(f32[640]{0:T(1024)} %copy-done.70) | copy-start | bytes 7684
  509.8 30.8 %copy-start.73 = (f32[640]{0:T(1024)S(1)}, f32[640]{0:T(1024)}, u32[]{:S(2)}) copy-start(f32[640]{0:T(1024)} %copy-done.72) | copy-start | bytes 7684
  534.8 5.8 collective-permute-start.1
  537.1 135.4 %all-reduce.72.cloned.1.call-start = ((), (), s32[]{:S(2)}) async-start(), calls=%async_computation.22 | async-start | bytes 6553600 | tf_op jit(solution)/shard_map/psum | solution.py:125
  548.3 190.8 %reduce-scatter.21.cloned.1.call-start = ((), (), s32[]{:S(2)}) async-start(), calls=%async_computation.16 | async-start | bytes 737280 | tf_op jit(solution)/shard_map/reduce_scatter | solution.py:198
  553.0 4.2 copy-start.46
  557.2 247.5 %reduce-scatter.19.cloned.1.call-start = ((), (), s32[]{:S(2)}) async-start(), calls=%async_computation.15 | async-start | bytes 737280 | tf_op jit(solution)/shard_map/reduce_scatter | solution.py:197
  560.9 4.3 copy-start.9
  565.1 364.7 %reduce-scatter.23.cloned.1.call-start = ((), (), s32[]{:S(2)}) async-start(), calls=%async_computation.17 | async-start | bytes 7372800 | tf_op jit(solution)/shard_map/reduce_scatter | solution.py:200
  569.2 485.8 %reduce-scatter.17.cloned.1.call-start = ((), (), s32[]{:S(2)}) async-start(), calls=%async_computation.14 | async-start | bytes 7372800 | tf_op jit(solution)/shard_map/reduce_scatter | solution.py:194
  574.4 605.7 %reduce-scatter.15.cloned.1.call-start = ((), (), s32[]{:S(2)}) async-start(), calls=%async_computation.13 | async-start | bytes 7372800 | tf_op jit(solution)/shard_map/reduce_scatter | solution.py:193
  579.4 928.2 %reduce-scatter.29.cloned.1.call-start = ((), (), s32[]{:S(2)}) async-start(), calls=%async_computation.20 | async-start | bytes 22118400 | tf_op jit(solution)/shard_map/reduce_scatter | solution.py:204
  589.1 1245.7 %reduce-scatter.27.cloned.1.call-start = ((), (), s32[]{:S(2)}) async-start(), calls=%async_computation.19 | async-start | bytes 22118400 | tf_op jit(solution)/shard_map/reduce_scatter | solution.py:203
  598.6 1563.4 %reduce-scatter.25.cloned.1.call-start = ((), (), s32[]{:S(2)}) async-start(), calls=%async_computation.18 | async-start | bytes 22118400 | tf_op jit(solution)/shard_map/reduce_scatter | solution.py:202
  608.1 66.3 %copy-start.63 = (f32[2560]{0:T(1024)S(1)}, f32[2560]{0:T(1024)}, u32[]{:S(2)}) copy-start(f32[2560]{0:T(1024)} %get-tuple-element.241) | copy-start | bytes 30724
  714.3 1447.8 %copy-start.1 = (bf16[2560,640]{1,0:T(8,128)(2,1)S(1)}, bf16[2560,640]{1,0:T(8,128)(2,1)}, u32[]{:S(2)}) copy-start(bf16[2560,640]{1,0:T(8,128)(2,1)} %param.22) | copy-start | bytes 9830404
  (54 other events, 99.0 us)
Sparse Core Ops, SparseCore 0:
  181.8 42.6 all-reduce.67
  256.3 43.9 all-reduce.69
  502.8 28.2 reduce-scatter.12
  537.2 63.3 reduce-scatter.30
  602.8 69.6 all-reduce.71
  676.2 62.8 reduce-scatter.20
  743.0 61.7 reduce-scatter.18
  808.9 120.8 reduce-scatter.22
  934.0 120.9 reduce-scatter.16
  1059.0 120.9 reduce-scatter.14
  1184.5 323.0 reduce-scatter.28
  1512.0 322.7 reduce-scatter.26
  1839.3 322.7 reduce-scatter.24
where the time goes:
time: 2180 us; the launch traced here: 2170 us
  waiting for transfers between devices  1600 us (73%)
  local copies, waits for them, and re-layouts  193 us (9%)
  blocking collectives  138 us (6%)
  other arithmetic  115 us (5%)
  matrix products  101 us (5%)
    reduce_scatter x1, waiting for transfers between devices, per_device(): lax.psum_scatter(g_down, 'seq', scatter_dimension=1, tiled=True)  328 us
    reduce_scatter x1, waiting for transfers between devices, per_device(): lax.psum_scatter(g_gate, 'seq', scatter_dimension=0, tiled=True)  327 us
    reduce_scatter x1, waiting for transfers between devices, per_device(): lax.psum_scatter(g_up, 'seq', scatter_dimension=0, tiled=True)  327 us
    reduce_scatter x1, waiting for transfers between devices, per_device(): lax.psum_scatter(g_y, 'seq', scatter_dimension=0, tiled=True)  125 us
    reduce_scatter x1, waiting for transfers between devices, per_device(): lax.psum_scatter(g_x, 'seq', scatter_dimension=0, tiled=True)  125 us
    reduce_scatter x1, waiting for transfers between devices, per_device(): lax.psum_scatter(g_out, 'seq', scatter_dimension=1, tiled=True)  125 us
    dot_general x24, matrix products, bdot(): return jnp.dot(left, right, preferred_element_type=jnp.float32)  101 us
    all_gather x3, blocking collectives, carried_in(): pieces = jax.tree.map(lambda part: lax.all_gather(part, axis), value)  91.7 us
  transfers between devices with their start and end apart: 15, of which 13 were waited for; matrix products, arithmetic and copies ran while one was open for 5% of the time, Pallas kernels for 0%

commit v1 on v0

v1 whole, which is shorter than its diff:
```python
import functools

import jax
import jax.numpy as jnp
from jax import lax
from jax.experimental import pallas as pl
from jax.experimental.pallas import tpu as pltpu
from jax.sharding import PartitionSpec as P


EPS = 1e-06
GELU_K = 0.7978845608028654
GELU_C = 0.044715
MIB = 1024 * 1024
SMALL_VMEM = 32 * MIB


def bdot(left, right):
    return jnp.dot(left, right, preferred_element_type=jnp.float32)


def tdot(left, right):
    return lax.dot_general(
        left, right, (((0,), (0,)), ((), ())), preferred_element_type=jnp.float32
    )


def dot_t(left, right):
    return lax.dot_general(
        left, right, (((1,), (1,)), ((), ())), preferred_element_type=jnp.float32
    )


def gelu_parts(values):
    square = values * values
    t = jnp.tanh(values * (GELU_K + (GELU_K * GELU_C) * square))
    half = 0.5 + 0.5 * t
    bend = values * (0.5 * GELU_K + (1.5 * GELU_K * GELU_C) * square)
    return values * half, half + bend * (1.0 - t * t)


def swap(value, axis, bit):
    size = lax.axis_size(axis)
    return lax.ppermute(value, axis, [(i, i ^ bit) for i in range(size)])


def shifted(value, axis, by):
    size = lax.axis_size(axis)
    return lax.ppermute(value, axis, [(i, i + by) for i in range(size) if 0 <= i + by < size])


def scan_rows(reverse, a_at, u_at, rows, store):
    groups = rows // 8
    carry_p = carry_h = None
    for step in range(groups):
        at = (groups - 1 - step if reverse else step) * 8
        a = a_at(at)
        u = u_at(at)
        row = lax.broadcasted_iota(jnp.int32, a.shape, 0)
        for k in (1, 2, 4):
            shift = 8 - k if reverse else k
            valid = row < 8 - k if reverse else row >= k
            a_far = jnp.where(valid, pltpu.roll(a, shift, 0), 1.0)
            u_far = jnp.where(valid, pltpu.roll(u, shift, 0), 0.0)
            u = u + a * u_far
            a = a * a_far
        if carry_p is not None:
            u = u + a * carry_h
            a = a * carry_p
        store(at, a, u)
        end = 0 if reverse else 7
        carry_p = jnp.broadcast_to(a[end : end + 1, :], a.shape)
        carry_h = jnp.broadcast_to(u[end : end + 1, :], a.shape)
    return carry_p[0:1], carry_h[0:1]


def head_blocks(odd, local_w, head):
    rest = local_w % head
    full = local_w // head
    if odd:
        blocks = [(0, rest, [(0, rest, "far", 0, rest), (rest, head, "own", 0, rest)])]
        first = rest
    else:
        at = full * head
        blocks = [
            (at, local_w, [(0, rest, "own", at, local_w), (rest, head, "far", 0, rest)])
        ]
        first = 0
    for j in range(full):
        lo = first + j * head
        blocks.append((lo, lo + head, [(0, head, "own", lo, lo + head)]))
    return blocks


def either(odd_ref, body):
    odd = odd_ref[0]

    @pl.when(odd == 0)
    def _():
        body(0)

    @pl.when(odd == 1)
    def _():
        body(1)


def norm_rows(low):
    value = low.astype(jnp.float32)
    r = lax.rsqrt(jnp.mean(value * value, axis=-1, keepdims=True) + EPS)
    return r, value * r


def softplus(value):
    e = jnp.exp(-jnp.abs(value))
    series = 1.0 / 9.0
    for k in (8.0, 7.0, 6.0, 5.0, 4.0, 3.0, 2.0, 1.0):
        series = 1.0 / k - e * series
    return jnp.maximum(value, 0.0) + jnp.where(e < 0.125, e * series, jnp.log(1.0 + e))


def in_hbm(*values):
    return [pltpu.with_memory_space_constraint(v, pltpu.HBM) for v in values]


def kept(shape, dtype):
    return pltpu.HBM(shape, dtype)


def begin(*copies):
    for copy in copies:
        copy.start()
    return copies


def front_kernel(
    odd_ref, tail_ref, x_hbm, gain_hbm, xw_hbm, yw_hbm, cw_hbm, cb_hbm, decay_hbm,
    conv_ref, low_ref, gated_ref, far_ref, soft_ref,
    normed_hbm, r_hbm, pad_hbm, slope_hbm, sig_hbm, conv_hbm, low_hbm, gated_hbm, soft_hbm,
    held, y_s, x_s, gain_s, xw_s, yw_s, cw_s, cb_s, decay_s, r_ref, pad_ref, slope_ref, sig_ref,
    sems, out_sems,
):
    rows = x_s.shape[0]
    steps, tk, local_w = xw_s.shape
    rest = far_ref.shape[1]
    copy = pltpu.make_async_copy
    x_copy, gain_copy = begin(
        copy(x_hbm, x_s, sems.at[0]), copy(gain_hbm, gain_s, sems.at[1])
    )
    weights = [
        begin(
            copy(xw_hbm.at[k * tk : (k + 1) * tk, :], xw_s.at[k], sems.at[5 + 2 * k]),
            copy(yw_hbm.at[k * tk : (k + 1) * tk, :], yw_s.at[k], sems.at[6 + 2 * k]),
        )
        for k in range(steps)
    ]
    last = begin(
        copy(cw_hbm, cw_s, sems.at[2]),
        copy(cb_hbm, cb_s, sems.at[3]),
        copy(decay_hbm, decay_s, sems.at[4]),
    )
    x_copy.wait()
    gain_copy.wait()
    gain = gain_s[...].reshape(1, gain_s.shape[0])
    r, n = norm_rows(x_s[...])
    r_ref[...] = r
    held[0:rows, :] = (n * gain).astype(jnp.bfloat16)
    outs = list(
        begin(
            copy(held.at[0:rows, :], normed_hbm, out_sems.at[0]),
            copy(r_ref, r_hbm, out_sems.at[1]),
        )
    )
    _, n = norm_rows(tail_ref[...])
    held[rows : rows + 8, :] = (n * gain).astype(jnp.bfloat16)
    pad_ref[...] = jnp.zeros_like(pad_ref)
    y_s[...] = jnp.zeros_like(y_s)
    for k, pair in enumerate(weights):
        at = slice(k * tk, (k + 1) * tk)
        for part in pair:
            part.wait()
        both = bdot(held[:, at], xw_s[k])
        pad_ref[0:8, :] += both[rows : rows + 8]
        pad_ref[8 : rows + 8, :] += both[0:rows]
        y_s[...] += bdot(held[0:rows, at], yw_s[k])
    outs += begin(copy(pad_ref, pad_hbm, out_sems.at[2]))
    for part in last:
        part.wait()
    param = decay_s[...].reshape(1, local_w)
    soft_ref[...] = softplus(param)
    sig_ref[...] = jax.nn.sigmoid(param)
    conv = cb_s[...].reshape(1, local_w) + cw_s[3:4, :] * pad_ref[8 : rows + 8, :]
    for offset in range(3):
        taps = pad_ref[5 + offset : 5 + offset + rows, :]
        conv = conv + cw_s[offset : offset + 1, :] * taps
    conv_ref[...] = conv
    low = conv.astype(jnp.bfloat16)
    low_ref[...] = low
    outs += begin(
        copy(conv_ref, conv_hbm, out_sems.at[3]),
        copy(low_ref, low_hbm, out_sems.at[4]),
        copy(sig_ref, sig_hbm, out_sems.at[5]),
        copy(soft_ref, soft_hbm, out_sems.at[6]),
    )

    def body(odd):
        lo = 0 if odd else local_w - rest
        far_ref[...] = low[:, lo : lo + rest]

    either(odd_ref, body)
    gelu, slope = gelu_parts(y_s[...])
    gated_ref[...] = gelu
    slope_ref[...] = slope
    outs += begin(
        copy(gated_ref, gated_hbm, out_sems.at[7]), copy(slope_ref, slope_hbm, out_sems.at[8])
    )
    for part in outs:
        part.wait()


def front(odd, x_low, tail, gain, xw, yw, cw, cb, decay_param, rest):
    rows, width = x_low.shape
    local_w = xw.shape[1]
    tk = 512
    steps = width // tk
    f32, bf16 = jnp.float32, jnp.bfloat16
    wide = jax.ShapeDtypeStruct((rows, local_w), f32)
    vmem = pl.BlockSpec(memory_space=pltpu.VMEM)
    hbm = pl.BlockSpec(memory_space=pltpu.HBM)
    line = jax.ShapeDtypeStruct((1, local_w), f32)
    return pl.pallas_call(
        front_kernel,
        in_specs=[pl.BlockSpec(memory_space=pltpu.SMEM), vmem] + [hbm] * 7,
        out_specs=[vmem] * 5 + [hbm] * 9,
        out_shape=(
            wide,
            jax.ShapeDtypeStruct((rows, local_w), bf16),
            wide,
            jax.ShapeDtypeStruct((rows, rest), bf16),
            line,
            kept((rows, width), bf16),
            kept((rows, 1), f32),
            kept((rows + 8, local_w), f32),
            kept((rows, local_w), f32),
            kept((1, local_w), f32),
            kept((rows, local_w), f32),
            kept((rows, local_w), bf16),
            kept((rows, local_w), f32),
            kept((1, local_w), f32),
        ),
        scratch_shapes=[
            pltpu.VMEM((rows + 8, width), bf16),
            pltpu.VMEM((rows, local_w), f32),
            pltpu.VMEM((rows, width), bf16),
            pltpu.VMEM((width,), f32),
            pltpu.VMEM((steps, tk, local_w), bf16),
            pltpu.VMEM((steps, tk, local_w), bf16),
            pltpu.VMEM((4, local_w), f32),
            pltpu.VMEM((local_w,), f32),
            pltpu.VMEM((local_w,), f32),
            pltpu.VMEM((rows, 1), f32),
            pltpu.VMEM((rows + 8, local_w), f32),
            pltpu.VMEM((rows, local_w), f32),
            pltpu.VMEM((1, local_w), f32),
            pltpu.SemaphoreType.DMA((5 + 2 * steps,)),
            pltpu.SemaphoreType.DMA((9,)),
        ],
        cost_estimate=pl.CostEstimate(
            flops=4 * rows * width * local_w,
            bytes_accessed=4 * width * local_w + 4 * rows * width,
            transcendentals=rows * local_w,
        ),
        compiler_params=pltpu.CompilerParams(vmem_limit_bytes=SMALL_VMEM),
        name="front",
    )(odd, tail, *in_hbm(x_low, gain, xw, yw, cw, cb, decay_param))


def small_call(kernel, outs, smem, *args):
    vmem = pl.BlockSpec(memory_space=pltpu.VMEM)
    scalars = [pl.BlockSpec(memory_space=pltpu.SMEM)] * len(smem)
    size = sum(a.size for a in args)
    return pl.pallas_call(
        kernel,
        in_specs=scalars + [vmem] * len(args),
        out_specs=[vmem] * len(outs),
        out_shape=tuple(jax.ShapeDtypeStruct(shape, dtype) for shape, dtype in outs),
        cost_estimate=pl.CostEstimate(flops=8 * size, bytes_accessed=8 * size, transcendentals=0),
        compiler_params=pltpu.CompilerParams(vmem_limit_bytes=SMALL_VMEM // 2),
    )(*smem, *args)


def half_call(kernel, odd, whole_rows, args, outs, held=()):
    spec = lambda a: pl.BlockSpec(a.shape, lambda i, odd_ref: (0,) * a.ndim)
    cut_spec = lambda a: pl.BlockSpec(
        (a.shape[0] // 2, a.shape[1]), lambda i, odd_ref: (odd_ref[0], 0)
    )
    size = sum(a.size for a in args)
    return pl.pallas_call(
        kernel,
        grid_spec=pltpu.PrefetchScalarGridSpec(
            num_scalar_prefetch=1,
            grid=(1,),
            in_specs=[cut_spec(a) for a in whole_rows] + [spec(a) for a in (*args, *held)],
            out_specs=[spec(jax.ShapeDtypeStruct(*o)) for o in outs],
        ),
        out_shape=tuple(kept(shape, dtype) for shape, dtype in outs),
        cost_estimate=pl.CostEstimate(flops=8 * size, bytes_accessed=8 * size, transcendentals=0),
        compiler_params=pltpu.CompilerParams(vmem_limit_bytes=SMALL_VMEM // 2),
    )(odd, *in_hbm(*whole_rows), *args, *in_hbm(*held))


def one_less_square(log_a, a):
    y = 2.0 * log_a
    series = 1.0 + y * (1.0 / 7.0)
    for k in (6.0, 5.0, 4.0, 3.0, 2.0):
        series = 1.0 + y * (1.0 / k) * series
    return jnp.where(y > -0.25, -y * series, 1.0 - a * a)


def gates_kernel(
    odd_ref, conv_ref, low_ref, far_ref, wx_ref, wa_ref, soft_ref,
    prod_ref, state_ref, total_ref, gx_hbm, ga_hbm, decay_hbm, mult_hbm, far_hbm, total_hbm,
    gx_ref, ga_ref, decay_ref, mult_ref, sems,
):
    rows, local_w = conv_ref.shape
    copy = pltpu.make_async_copy
    outs = list(begin(copy(far_ref, far_hbm, sems.at[0])))
    head = wx_ref.shape[0]

    def body(odd):
        src = {"own": low_ref, "far": far_ref}
        for lo, hi, parts in head_blocks(odd, local_w, head):
            for w_ref, g_ref in ((wx_ref, gx_ref), (wa_ref, ga_ref)):
                acc = None
                for r0, r1, name, s0, s1 in parts:
                    term = bdot(src[name][:, s0:s1], w_ref[r0:r1, lo:hi])
                    acc = term if acc is None else acc + term
                g_ref[:, lo:hi] = jax.nn.sigmoid(acc)

    either(odd_ref, body)
    outs += begin(copy(gx_ref, gx_hbm, sems.at[1]), copy(ga_ref, ga_hbm, sems.at[2]))
    log_decay = -8.0 * soft_ref[...] * ga_ref[...]
    decay = jnp.exp(log_decay)
    mult = jnp.sqrt(one_less_square(log_decay, decay))
    decay_ref[...] = decay
    mult_ref[...] = mult
    outs += begin(copy(decay_ref, decay_hbm, sems.at[3]), copy(mult_ref, mult_hbm, sems.at[4]))
    state_ref[...] = conv_ref[...] * gx_ref[...] * mult

    def store(at, p, h):
        prod_ref[at : at + 8, :] = p
        state_ref[at : at + 8, :] = h

    prod, end = scan_rows(
        False, lambda at: decay_ref[at : at + 8, :], lambda at: state_ref[at : at + 8, :], rows, store
    )
    total_ref[0:1, :] = prod
    total_ref[1:2, :] = end
    outs += begin(copy(total_ref, total_hbm, sems.at[5]))
    for part in outs:
        part.wait()


def gates(odd, conv, low, far, wx, wa, soft):
    rows, local_w = conv.shape
    head = wx.shape[0]
    f32 = jnp.float32
    wide = jax.ShapeDtypeStruct((rows, local_w), f32)
    vmem = pl.BlockSpec(memory_space=pltpu.VMEM)
    hbm = pl.BlockSpec(memory_space=pltpu.HBM)
    return pl.pallas_call(
        gates_kernel,
        in_specs=[pl.BlockSpec(memory_space=pltpu.SMEM)] + [vmem] * 6,
        out_specs=[vmem] * 3 + [hbm] * 6,
        out_shape=(wide, wide, jax.ShapeDtypeStruct((2, local_w), f32))
        + (kept((rows, local_w), f32),) * 4
        + (kept(far.shape, far.dtype), kept((2, local_w), f32)),
        scratch_shapes=[pltpu.VMEM((rows, local_w), f32)] * 4 + [pltpu.SemaphoreType.DMA((6,))],
        cost_estimate=pl.CostEstimate(
            flops=4 * rows * head * local_w + 60 * rows * local_w,
            bytes_accessed=40 * rows * local_w,
            transcendentals=6 * rows * local_w,
        ),
        compiler_params=pltpu.CompilerParams(vmem_limit_bytes=SMALL_VMEM),
        name="gates",
    )(odd, conv, low, far, wx, wa, soft)


def mix_kernel(
    odd_ref, state_in_ref, prod_ref, state_ref, gated_ref, w_hbm,
    mixed_ref, keep_ref, send_ref, hidden_hbm, state_in_hbm, w_s, sems, hidden_ref, out_sems,
):
    steps, _, tn = w_s.shape
    half = keep_ref.shape[0]
    copies = begin(
        *[
            pltpu.make_async_copy(w_hbm.at[:, j * tn : (j + 1) * tn], w_s.at[j], sems.at[j])
            for j in range(steps)
        ]
    )
    hidden = state_ref[...] + prod_ref[...] * state_in_ref[...]
    hidden_ref[...] = hidden
    outs = begin(
        pltpu.make_async_copy(hidden_ref, hidden_hbm, out_sems.at[0]),
        pltpu.make_async_copy(state_in_ref, state_in_hbm, out_sems.at[1]),
    )
    mixed_ref[...] = (hidden * gated_ref[...]).astype(jnp.bfloat16)
    for copy in copies:
        copy.wait()

    @pl.loop(0, steps)
    def _(j):
        at = pl.ds(pl.multiple_of(j * tn, tn), tn)
        full = bdot(mixed_ref[...], w_s[j])

        def body(odd):
            keep_ref[:, at] = full[odd * half : odd * half + half]
            send_ref[:, at] = full[(1 - odd) * half : (1 - odd) * half + half]

        either(odd_ref, body)

    for copy in outs:
        copy.wait()


def mix(odd, state_in, prod, state, gated, w):
    rows, local_w = prod.shape
    width = w.shape[1]
    tn = 512
    vmem = pl.BlockSpec(memory_space=pltpu.VMEM)
    part = jax.ShapeDtypeStruct((rows // 2, width), jnp.float32)
    return pl.pallas_call(
        mix_kernel,
        in_specs=[pl.BlockSpec(memory_space=pltpu.SMEM)]
        + [vmem] * 4
        + [pl.BlockSpec(memory_space=pltpu.HBM)],
        out_specs=[vmem] * 3 + [pl.BlockSpec(memory_space=pltpu.HBM)] * 2,
        out_shape=(
            jax.ShapeDtypeStruct((rows, local_w), jnp.bfloat16),
            part, part,
            kept((rows, local_w), jnp.float32),
            kept((1, local_w), jnp.float32),
        ),
        scratch_shapes=[
            pltpu.VMEM((width // tn, local_w, tn), jnp.bfloat16),
            pltpu.SemaphoreType.DMA((width // tn,)),
            pltpu.VMEM((rows, local_w), jnp.float32),
            pltpu.SemaphoreType.DMA((2,)),
        ],
        cost_estimate=pl.CostEstimate(
            flops=2 * rows * local_w * width,
            bytes_accessed=2 * local_w * width + 4 * rows * width,
            transcendentals=0,
        ),
        compiler_params=pltpu.CompilerParams(vmem_limit_bytes=SMALL_VMEM),
        name="mix",
    )(odd, state_in, prod, state, gated, *in_hbm(w))


def ffn_act(normed, d_act, gw_ref, uw_ref, rest_ref):
    tn = gw_ref.shape[1]
    main = tn // 256 * 256
    rest = bdot(normed, rest_ref[...])
    gate = jnp.concatenate([bdot(normed, gw_ref[:, 0:main]), rest[:, 0 : tn - main]], axis=1)
    up = jnp.concatenate([bdot(normed, uw_ref[:, 0:main]), rest[:, tn - main :]], axis=1)
    gelu, slope = gelu_parts(gate)
    act = (gelu * up).astype(jnp.bfloat16)
    d_gate = (d_act * up * slope).astype(jnp.bfloat16)
    d_up = (d_act * gelu).astype(jnp.bfloat16)
    return act, d_gate, d_up


def fill_rest(gw_ref, uw_ref, rest_s):
    tn = gw_ref.shape[1]
    main = tn // 256 * 256
    rest_s[:, 0 : tn - main] = gw_ref[:, main:tn]
    rest_s[:, tn - main :] = uw_ref[:, main:tn]


def start_kernel(odd_ref, cot_ref, share_ref, x_ref, own_ref, share_out, tail_ref):
    own_ref[...] = cot_ref[...]
    share_out[...] = share_ref[...]
    tail_ref[...] = x_ref[...]


def start(odd, cot, x_low, share):
    rows, width = cot.shape
    half = rows // 2
    part = half // share
    return pl.pallas_call(
        start_kernel,
        grid_spec=pltpu.PrefetchScalarGridSpec(
            num_scalar_prefetch=1,
            grid=(1,),
            in_specs=[
                pl.BlockSpec((half, width), lambda i, odd_ref: (odd_ref[0], 0)),
                pl.BlockSpec((part, width), lambda i, odd_ref: (odd_ref[0] * share + odd_ref[2], 0)),
                pl.BlockSpec((8, width), lambda i, odd_ref: (rows // 8 - 1, 0)),
            ],
            out_specs=[
                pl.BlockSpec((half, width), lambda i, odd_ref: (0, 0)),
                pl.BlockSpec((part, width), lambda i, odd_ref: (0, 0)),
                pl.BlockSpec((8, width), lambda i, odd_ref: (0, 0)),
            ],
        ),
        out_shape=(
            kept((half, width), cot.dtype),
            kept((part, width), cot.dtype),
            jax.ShapeDtypeStruct((8, width), x_low.dtype),
        ),
        compiler_params=pltpu.CompilerParams(vmem_limit_bytes=SMALL_VMEM // 2),
        name="start",
    )(odd, *in_hbm(cot, cot, x_low))


def braid_kernel(odd_ref, own_ref, far_ref, out_ref):
    part = own_ref.shape[0]
    second = odd_ref[2]
    out_ref[pl.ds(pl.multiple_of(second * part, 8), part), :] = own_ref[...]
    out_ref[pl.ds(pl.multiple_of((1 - second) * part, 8), part), :] = far_ref[...]


def braid(odd, own, far, blocks):
    rows, width = own.shape
    part = rows // blocks
    side = pl.BlockSpec((part, width), lambda i, odd_ref: (i, 0))
    return pl.pallas_call(
        braid_kernel,
        grid_spec=pltpu.PrefetchScalarGridSpec(
            num_scalar_prefetch=1,
            grid=(blocks,),
            in_specs=[side, side],
            out_specs=pl.BlockSpec((2 * part, width), lambda i, odd_ref: (i, 0)),
        ),
        out_shape=jax.ShapeDtypeStruct((2 * rows, width), own.dtype),
        cost_estimate=pl.CostEstimate(
            flops=0, bytes_accessed=8 * rows * width, transcendentals=0
        ),
        compiler_params=pltpu.CompilerParams(vmem_limit_bytes=SMALL_VMEM // 2),
        name="braid",
    )(odd, *in_hbm(own, far))


def d_act_kernel(odd_ref, c_ref, dw_ref, out_ref):
    half = c_ref.shape[0] // 2
    full = dot_t(c_ref[...], dw_ref[...])

    def body(odd):
        out_ref[0:half, :] = full[odd * half : odd * half + half]
        out_ref[half:, :] = full[(1 - odd) * half : (1 - odd) * half + half]

    either(odd_ref, body)


def own_d_act(odd, cot, dw):
    rows, width = cot.shape
    half = rows // 2
    local_f = dw.shape[0]
    tn = 640
    whole = pl.BlockSpec((rows, width), lambda j: (0, 0))
    return pl.pallas_call(
        d_act_kernel,
        grid=(local_f // tn,),
        in_specs=[
            pl.BlockSpec(memory_space=pltpu.SMEM), whole,
            pl.BlockSpec((tn, width), lambda j: (j, 0)),
        ],
        out_specs=pl.BlockSpec((2 * half, tn), lambda j: (0, j)),
        out_shape=jax.ShapeDtypeStruct((2 * half, local_f), jnp.float32),
        cost_estimate=pl.CostEstimate(
            flops=4 * half * width * local_f,
            bytes_accessed=2 * width * local_f,
            transcendentals=0,
        ),
        compiler_params=pltpu.CompilerParams(vmem_limit_bytes=SMALL_VMEM),
        name="own_d_act",
    )(odd, *in_hbm(cot, dw))


def ffn_own_kernel(
    nfar_ref, da_ref, n_hbm, gw_hbm, uw_hbm, keep_ref, send_ref, act_ref,
    n_s, rest_s, gw_s, uw_s, sems, n_sem,
):
    half = keep_ref.shape[0]
    steps, _, tn = gw_s.shape
    main = tn // 256 * 256
    (n_copy,) = begin(pltpu.make_async_copy(n_hbm, n_s.at[0:half, :], n_sem.at[0]))
    for j in range(steps):
        at = slice(j * tn, (j + 1) * tn)
        begin(
            pltpu.make_async_copy(gw_hbm.at[:, at], gw_s.at[j], sems.at[0, j]),
            pltpu.make_async_copy(uw_hbm.at[:, at], uw_s.at[j], sems.at[1, j]),
        )
    n_s[half:, :] = nfar_ref[...]
    keep_ref[...] = jnp.zeros_like(keep_ref)
    send_ref[...] = jnp.zeros_like(send_ref)
    n_copy.wait()

    @pl.loop(0, steps)
    def _(j):
        at = pl.ds(pl.multiple_of(j * tn, tn), tn)
        gw_ref, uw_ref = gw_s.at[j], uw_s.at[j]
        pltpu.make_async_copy(gw_hbm.at[:, at], gw_ref, sems.at[0, j]).wait()
        pltpu.make_async_copy(uw_hbm.at[:, at], uw_ref, sems.at[1, j]).wait()
        fill_rest(gw_ref, uw_ref, rest_s)
        act, d_gate, d_up = ffn_act(n_s[...], da_ref[:, at], gw_ref, uw_ref, rest_s)
        act_ref[:, at] = act
        d_rest = jnp.concatenate([d_gate[:, main:], d_up[:, main:]], axis=1)
        d_n = dot_t(d_gate[:, 0:main], gw_ref[:, 0:main])
        d_n = d_n + dot_t(d_up[:, 0:main], uw_ref[:, 0:main])
        d_n = d_n + dot_t(d_rest, rest_s[...])
        keep_ref[...] += d_n[0:half]
        send_ref[...] += d_n[half:]


def ffn_own(normed, normed_far, d_act, gw, uw):
    half, width = normed.shape
    rows = 2 * half
    local_f = gw.shape[1]
    tn = 640
    steps = local_f // tn
    vmem = pl.BlockSpec(memory_space=pltpu.VMEM)
    hbm = pl.BlockSpec(memory_space=pltpu.HBM)
    part = jax.ShapeDtypeStruct((half, width), jnp.float32)
    return pl.pallas_call(
        ffn_own_kernel,
        in_specs=[vmem] * 2 + [hbm] * 3,
        out_specs=[vmem] * 3,
        out_shape=(part, part, jax.ShapeDtypeStruct((rows, local_f), jnp.bfloat16)),
        scratch_shapes=[
            pltpu.VMEM((rows, width), jnp.bfloat16),
            pltpu.VMEM((width, 2 * (tn % 256)), jnp.bfloat16),
            pltpu.VMEM((steps, width, tn), jnp.bfloat16),
            pltpu.VMEM((steps, width, tn), jnp.bfloat16),
            pltpu.SemaphoreType.DMA((2, steps)),
            pltpu.SemaphoreType.DMA((1,)),
        ],
        cost_estimate=pl.CostEstimate(
            flops=8 * rows * width * local_f,
            bytes_accessed=4 * width * local_f,
            transcendentals=rows * local_f,
        ),
        compiler_params=pltpu.CompilerParams(vmem_limit_bytes=36 * MIB),
        name="ffn_own",
    )(normed_far, d_act, *in_hbm(normed, gw, uw))


def ffn_out_kernel(act_ref, dw_ref, keep_ref, send_ref):
    half = keep_ref.shape[0]
    out = bdot(act_ref[...], dw_ref[...])
    keep_ref[...] = out[0:half]
    send_ref[...] = out[half:]


def ffn_out(act, dw):
    rows, local_f = act.shape
    width = dw.shape[1]
    tn = 512
    part = pl.BlockSpec((rows // 2, tn), lambda j: (0, j))
    shape = jax.ShapeDtypeStruct((rows // 2, width), jnp.float32)
    return pl.pallas_call(
        ffn_out_kernel,
        grid=(width // tn,),
        in_specs=[
            pl.BlockSpec((rows, local_f), lambda j: (0, 0)),
            pl.BlockSpec((local_f, tn), lambda j: (0, j)),
        ],
        out_specs=[part, part],
        out_shape=(shape, shape),
        cost_estimate=pl.CostEstimate(
            flops=2 * rows * width * local_f,
            bytes_accessed=2 * width * local_f,
            transcendentals=0,
        ),
        compiler_params=pltpu.CompilerParams(vmem_limit_bytes=SMALL_VMEM),
        name="ffn_out",
    )(act, *in_hbm(dw))


def ffn_all_kernel(
    sub, span, place_ref, n_ref, nfar_ref, c_ref, cfar_ref, gw_ref, uw_ref, dw_ref,
    gg_ref, gu_ref, gd_ref, both, act_s, rest_s, nt_s, ct_s,
):
    rows = n_ref.shape[0]
    tn = gw_ref.shape[1]
    cols = gg_ref.shape[0]
    chunk = pl.program_id(1)
    fill_rest(gw_ref, uw_ref, rest_s)

    @pl.when(pl.program_id(0) == 0)
    def _():
        start = place_ref[1] * cols
        width = n_ref.shape[1]
        base = pl.multiple_of(jnp.minimum(start // 128 * 128, width - span), 128)
        row = lax.broadcasted_iota(jnp.int32, (cols, span), 0)
        col = lax.broadcasted_iota(jnp.int32, (cols, span), 1)
        pick = jnp.where(col == row + (start - base), 1.0, 0.0).astype(jnp.bfloat16)
        for to, pair in ((nt_s, (n_ref, nfar_ref)), (ct_s, (c_ref, cfar_ref))):
            for k, ref in enumerate(pair):
                turned_cols = dot_t(pick, ref[:, pl.ds(base, span)])
                to[chunk, :, k * rows : (k + 1) * rows] = turned_cols.astype(jnp.bfloat16)

    for base, n, c in ((0, n_ref, c_ref), (rows, nfar_ref, cfar_ref)):
        for i in range(0, rows, sub):
            to = slice(base + i, base + i + sub)
            d_act = dot_t(c[i : i + sub, :], dw_ref[...])
            act, d_gate, d_up = ffn_act(n[i : i + sub, :], d_act, gw_ref, uw_ref, rest_s)
            act_s[to, :] = act
            both[to, 0:tn] = d_gate
            both[to, tn : 2 * tn] = d_up

    grads = bdot(nt_s[chunk], both[...])
    down = bdot(ct_s[chunk], act_s[...])
    first = pl.program_id(1) == 0

    @pl.when(first)
    def _():
        gg_ref[...] = grads[:, 0:tn]
        gu_ref[...] = grads[:, tn:]
        gd_ref[...] = down

    @pl.when(jnp.logical_not(first))
    def _():
        gg_ref[...] += grads[:, 0:tn]
        gu_ref[...] += grads[:, tn:]
        gd_ref[...] += down


def ffn_all(place, cols, normed, normed_far, cot, cot_far, gw, uw, dw):
    rows, width = cot.shape
    local_f = gw.shape[1]
    skip = max(k * cols % 128 for k in range(width // cols))
    span = -(-(cols + skip) // 128) * 128
    tn = 640
    sub = 320
    chunk = rows if rows <= 640 else sub
    once = pl.Buffered(1) if chunk == rows else pl.Buffered(2)
    tall = pl.BlockSpec((chunk, width), lambda j, r: (r, 0), pipeline_mode=once)
    col = pl.BlockSpec((width, tn), lambda j, r: (0, j))
    out_col = pl.BlockSpec((cols, tn), lambda j, r: (0, j))
    wide = jax.ShapeDtypeStruct((cols, local_f), jnp.float32)
    return pl.pallas_call(
        functools.partial(ffn_all_kernel, sub, span),
        grid=(local_f // tn, rows // chunk),
        in_specs=[pl.BlockSpec(memory_space=pltpu.SMEM)]
        + [tall] * 4
        + [col, col, pl.BlockSpec((tn, width), lambda j, r: (j, 0))],
        out_specs=[out_col] * 3,
        out_shape=(wide,) * 3,
        scratch_shapes=[
            pltpu.VMEM((2 * chunk, 2 * tn), jnp.bfloat16),
            pltpu.VMEM((2 * chunk, tn), jnp.bfloat16),
            pltpu.VMEM((width, 2 * (tn % 256)), jnp.bfloat16),
            pltpu.VMEM((rows // chunk, cols, 2 * chunk), jnp.bfloat16),
            pltpu.VMEM((rows // chunk, cols, 2 * chunk), jnp.bfloat16),
        ],
        cost_estimate=pl.CostEstimate(
            flops=12 * rows * width * local_f + 12 * rows * cols * local_f,
            bytes_accessed=6 * width * local_f + 8 * rows * width + 12 * cols * local_f,
            transcendentals=2 * rows * local_f,
        ),
        compiler_params=pltpu.CompilerParams(vmem_limit_bytes=58 * 1024 * 1024),
        name="ffn_all",
    )(place, normed, normed_far, cot, cot_far, gw, uw, dw)


def sums_kernel(cols, half, packed_ref, gx_ref, ga_ref, vec_ref, gain_ref):
    blocks, _, span = packed_ref.shape
    total = packed_ref[0, half:, :].astype(jnp.float32)
    for k in range(1, blocks):
        total = total + packed_ref[k, half:, :].astype(jnp.float32)
    tall, local_w = gx_ref.shape
    pieces = local_w // span
    for g, ref in enumerate((gx_ref, ga_ref)):
        for q in range(pieces):
            at = (g * pieces + q) * tall
            ref[:, q * span : (q + 1) * span] = total[at : at + tall]
    small = total[2 * pieces * tall :]
    thin = vec_ref.shape[1]
    vec_ref[...] = small[:, 0:thin] + small[:, cols : cols + thin]
    gain_ref[...] = jnp.broadcast_to(small[6:7] + small[7:8], gain_ref.shape)


def token_grads_kernel(
    half, odd_ref, mixed_ref, mfar_ref, b_ref, bfar_ref, own_ref, far_ref, out_ref, y_ref, x_ref
):
    rows, local_w = mixed_ref.shape
    span = own_ref.shape[2]
    cols = span // 2
    out = both = None
    for m, b, p in ((mixed_ref, b_ref, own_ref), (mfar_ref, bfar_ref, far_ref)):
        side = p[:, 0:half, :].reshape(rows, span)
        term = tdot(side[:, cols:], m[...])
        out = term if out is None else out + term
        term = tdot(side[:, 0:cols], b[...])
        both = term if both is None else both + term
    out_ref[...] = out
    y_ref[...] = both[:, 0:local_w]
    x_ref[...] = both[:, local_w:]


def token_grads(odd, gathered, first, branches, packed, packed_far, half, local_w):
    rows = gathered.shape[0]
    span = packed.shape[2]
    cols = span // 2
    window = lambda tile, at, flip: pl.BlockSpec(
        (rows, tile), lambda i, odd_ref: (0, at + (1 - odd_ref[0] if flip else odd_ref[0]))
    )
    whole = pl.BlockSpec(packed.shape, lambda i, odd_ref: (0, 0, 0))
    out = pl.BlockSpec((cols, local_w), lambda i, odd_ref: (0, 0))
    return pl.pallas_call(
        functools.partial(token_grads_kernel, half),
        grid_spec=pltpu.PrefetchScalarGridSpec(
            num_scalar_prefetch=1,
            grid=(1,),
            in_specs=[
                window(local_w, first, False), window(local_w, first, True),
                window(2 * local_w, 0, False), window(2 * local_w, 0, True), whole, whole,
            ],
            out_specs=[out] * 3,
        ),
        out_shape=(jax.ShapeDtypeStruct((cols, local_w), jnp.float32),) * 3,
        cost_estimate=pl.CostEstimate(
            flops=12 * rows * cols * local_w, bytes_accessed=16 * rows * local_w, transcendentals=0
        ),
        compiler_params=pltpu.CompilerParams(vmem_limit_bytes=58 * MIB),
        name="token_grads",
    )(odd, *in_hbm(gathered, gathered, branches, branches, packed, packed_far))


def back_kernel(
    odd_ref, own_ref, far_ref, hidden_ref, gated_ref, slope_ref, decay_ref, prod_ref, w_hbm,
    dy_ref, lam_ref, after_ref, total_ref, acc, d_s, w_s, sems,
):
    half = own_ref.shape[0]
    rows = 2 * half
    steps, _, tk = w_s.shape
    copies = begin(
        *[
            pltpu.make_async_copy(w_hbm.at[:, j * tk : (j + 1) * tk], w_s.at[j], sems.at[j])
            for j in range(steps)
        ]
    )
    d_s[0:half, :] = own_ref[...]
    d_s[half:, :] = far_ref[...]
    acc[...] = jnp.zeros_like(acc)
    for copy in copies:
        copy.wait()

    @pl.loop(0, steps)
    def _(j):
        acc[...] += dot_t(d_s[:, pl.ds(pl.multiple_of(j * tk, tk), tk)], w_s[j])

    def body(odd):
        for to, at in ((odd * half, 0), ((1 - odd) * half, half)):
            rows_to = slice(to, to + half)
            d_mixed = acc[at : at + half, :]
            dy_ref[rows_to, :] = (
                d_mixed * hidden_ref[rows_to, :] * slope_ref[rows_to, :]
            ).astype(jnp.bfloat16)
            lam_ref[rows_to, :] = d_mixed * gated_ref[rows_to, :]

    either(odd_ref, body)

    def next_decay(at):
        if at + 8 < rows:
            return decay_ref[at + 1 : at + 9, :]
        last = pltpu.roll(decay_ref[at : at + 8, :], 7, 0)
        row = lax.broadcasted_iota(jnp.int32, last.shape, 0)
        return jnp.where(row == 7, 1.0, last)

    def store(at, p, h):
        after_ref[at : at + 8, :] = p
        lam_ref[at : at + 8, :] = h

    _, first = scan_rows(True, next_decay, lambda at: lam_ref[at : at + 8, :], rows, store)
    total_ref[0:1, :] = prod_ref[0:1, :]
    total_ref[1:2, :] = decay_ref[0:1, :] * first


def back(odd, own, far, w, hidden, gated, slope, decay, prod):
    half, width = own.shape
    rows = 2 * half
    local_w = w.shape[0]
    tk = 512
    vmem = pl.BlockSpec(memory_space=pltpu.VMEM)
    wide = jax.ShapeDtypeStruct((rows, local_w), jnp.float32)
    return pl.pallas_call(
        back_kernel,
        in_specs=[pl.BlockSpec(memory_space=pltpu.SMEM)]
        + [vmem] * 7
        + [pl.BlockSpec(memory_space=pltpu.HBM)],
        out_specs=[vmem] * 4,
        out_shape=(
            jax.ShapeDtypeStruct((rows, local_w), jnp.bfloat16), wide, wide,
            jax.ShapeDtypeStruct((2, local_w), jnp.float32),
        ),
        scratch_shapes=[
            pltpu.VMEM((rows, local_w), jnp.float32),
            pltpu.VMEM((rows, width), jnp.bfloat16),
            pltpu.VMEM((width // tk, local_w, tk), jnp.bfloat16),
            pltpu.SemaphoreType.DMA((width // tk,)),
        ],
        cost_estimate=pl.CostEstimate(
            flops=2 * rows * width * local_w,
            bytes_accessed=2 * width * local_w + 30 * rows * local_w,
            transcendentals=0,
        ),
        compiler_params=pltpu.CompilerParams(vmem_limit_bytes=SMALL_VMEM),
        name="back",
    )(odd, own, far, hidden, gated, slope, decay, prod, *in_hbm(w))


def gates_back_kernel(
    odd_ref, returned_ref, state_in_ref, lam_ref, after_ref, hidden_ref, decay_ref, mult_ref,
    conv_ref, low_ref, far_ref, gx_ref, ga_ref, wx_ref, wa_ref, soft_ref, sig_ref,
    dconv_ref, dfar_ref, halo_ref, gwx_ref, gwa_ref, gdecay_ref, dgx_s, dga_s,
):
    _, local_w = conv_ref.shape
    head = wx_ref.shape[0]
    lam = lam_ref[...] + after_ref[...] * returned_ref[...]
    decay, mult, gx, ga = decay_ref[...], mult_ref[...], gx_ref[...], ga_ref[...]
    conv = conv_ref[...]
    before = pltpu.roll(hidden_ref[...], 1, 0)
    row = lax.broadcasted_iota(jnp.int32, before.shape, 0)
    before = jnp.where(row == 0, state_in_ref[...], before)
    lam_gx = lam * gx
    d_log = lam * before * decay - lam_gx * conv * decay * decay / mult
    scaled = d_log * -8.0 * ga
    gdecay_ref[...] = jnp.sum(scaled, axis=0, keepdims=True) * sig_ref[...]
    dga_s[...] = (scaled * soft_ref[...] * (1.0 - ga)).astype(jnp.bfloat16)
    lam_gx_m = lam_gx * mult
    dgx_s[...] = (lam_gx_m * conv * (1.0 - gx)).astype(jnp.bfloat16)
    dconv_ref[...] = lam_gx_m

    def body(odd):
        src = {"own": low_ref, "far": far_ref}
        for lo, hi, parts in head_blocks(odd, local_w, head):
            d_x, d_a = dgx_s[:, lo:hi], dga_s[:, lo:hi]
            for r0, r1, name, s0, s1 in parts:
                piece = src[name][:, s0:s1]
                gwx_ref[r0:r1, lo:hi] = tdot(piece, d_x)
                gwa_ref[r0:r1, lo:hi] = tdot(piece, d_a)
                term = dot_t(d_x, wx_ref[r0:r1, lo:hi]) + dot_t(d_a, wa_ref[r0:r1, lo:hi])
                if name == "own":
                    dconv_ref[:, s0:s1] += term
                else:
                    dfar_ref[...] = term

    either(odd_ref, body)
    halo_ref[:, 0:local_w] = dconv_ref[0:8, :]
    halo_ref[:, local_w:] = dfar_ref[0:8, :]


def gates_back(odd, returned, state_in, lam, after, hidden, decay, mult, conv, low, far, gx, ga, wx, wa, soft, sig):
    rows, local_w = conv.shape
    head = wx.shape[0]
    f32 = jnp.float32
    vmem = pl.BlockSpec(memory_space=pltpu.VMEM)
    return pl.pallas_call(
        gates_back_kernel,
        in_specs=[pl.BlockSpec(memory_space=pltpu.SMEM)] + [vmem] * 16,
        out_specs=[vmem] * 6,
        out_shape=(
            jax.ShapeDtypeStruct((rows, local_w), f32),
            jax.ShapeDtypeStruct((rows, local_w % head), f32),
            jax.ShapeDtypeStruct((8, local_w + local_w % head), f32),
            jax.ShapeDtypeStruct((head, local_w), f32),
            jax.ShapeDtypeStruct((head, local_w), f32),
            jax.ShapeDtypeStruct((1, local_w), f32),
        ),
        scratch_shapes=[pltpu.VMEM((rows, local_w), jnp.bfloat16)] * 2,
        cost_estimate=pl.CostEstimate(
            flops=8 * rows * head * local_w + 40 * rows * local_w,
            bytes_accessed=44 * rows * local_w,
            transcendentals=rows * local_w,
        ),
        compiler_params=pltpu.CompilerParams(vmem_limit_bytes=SMALL_VMEM),
        name="gates_back",
    )(odd, returned, state_in, lam, after, hidden, decay, mult, conv, low, far, gx, ga, wx, wa, soft, sig)


def tail_kernel(
    odd_ref, dconv_ref, far_ref, later_ref, dy_ref, gdecay_ref, pad_hbm, cw_hbm, r_hbm, xw_hbm,
    yw_hbm, x_hbm, keep_ref, send_ref, branch_ref, vec_ref, mix_ref,
    ext, dx_s, pad_ref, cw_ref, r_ref, xw_s, yw_s, x_s, sems,
):
    rows, local_w = dconv_ref.shape
    rest = far_ref.shape[1]
    half = rows // 2
    steps, tn, _ = xw_s.shape
    copy = pltpu.make_async_copy
    early = begin(
        copy(pad_hbm, pad_ref, sems.at[0]), copy(cw_hbm, cw_ref, sems.at[1]),
        copy(r_hbm, r_ref, sems.at[2]),
    )
    weights = []
    for j in range(steps):
        at = slice(j * tn, (j + 1) * tn)
        weights += begin(
            copy(xw_hbm.at[at, :], xw_s.at[j], sems.at[3 + 3 * j]),
            copy(yw_hbm.at[at, :], yw_s.at[j], sems.at[4 + 3 * j]),
            copy(x_hbm.at[:, at], x_s.at[j], sems.at[5 + 3 * j]),
        )
    ext[0:rows, :] = dconv_ref[...]
    ext[rows : rows + 8, :] = later_ref[:, 0:local_w]

    def body(odd):
        lo = 0 if odd else local_w - rest
        ext[:, lo : lo + rest] += far_ref[...]

    either(odd_ref, body)
    for part in early:
        part.wait()
    d_conv = ext[0:rows, :]
    vec_ref[4:5, :] = jnp.sum(d_conv, axis=0, keepdims=True)
    vec_ref[5:6, :] = gdecay_ref[...]
    vec_ref[6:8, :] = jnp.zeros((2, local_w), jnp.float32)
    d_x = cw_ref[3:4, :] * d_conv
    for offset in range(4):
        shifted_in = pad_ref[5 + offset : 5 + offset + rows, :]
        vec_ref[offset : offset + 1, :] = jnp.sum(d_conv * shifted_in, axis=0, keepdims=True)
        if offset < 3:
            d_x = d_x + cw_ref[offset : offset + 1, :] * ext[3 - offset : 3 - offset + rows, :]
    dx_s[...] = d_x.astype(jnp.bfloat16)
    for k in (0, 1):
        rows_k = slice(k * half, (k + 1) * half)
        branch_ref[:, 2 * k * local_w : (2 * k + 1) * local_w] = dy_ref[rows_k, :]
        branch_ref[:, (2 * k + 1) * local_w : (2 * k + 2) * local_w] = dx_s[rows_k, :]
    for part in weights:
        part.wait()

    @pl.loop(0, steps)
    def _(j):
        at = pl.ds(pl.multiple_of(j * tn, tn), tn)
        full = dot_t(dx_s[...], xw_s[j]) + dot_t(dy_ref[...], yw_s[j])
        n_one = x_s[j].astype(jnp.float32) * r_ref[...]
        mix_ref[:, at] = jnp.sum(full * n_one, axis=0, keepdims=True)

        def split(odd):
            keep_ref[:, at] = full[odd * half : odd * half + half]
            send_ref[:, at] = full[(1 - odd) * half : (1 - odd) * half + half]

        either(odd_ref, split)


def tail(odd, dconv, far, later, pad, cw, dy, gdecay, xw, yw, x_low, r_one):
    rows, local_w = dconv.shape
    width = xw.shape[0]
    tn = 512
    steps = width // tn
    f32, bf16 = jnp.float32, jnp.bfloat16
    vmem = pl.BlockSpec(memory_space=pltpu.VMEM)
    hbm = pl.BlockSpec(memory_space=pltpu.HBM)
    part = jax.ShapeDtypeStruct((rows // 2, width), f32)
    return pl.pallas_call(
        tail_kernel,
        in_specs=[pl.BlockSpec(memory_space=pltpu.SMEM)] + [vmem] * 5 + [hbm] * 6,
        out_specs=[vmem] * 5,
        out_shape=(
            part, part,
            jax.ShapeDtypeStruct((rows // 2, 4 * local_w), bf16),
            jax.ShapeDtypeStruct((8, local_w), f32),
            jax.ShapeDtypeStruct((1, width), f32),
        ),
        scratch_shapes=[
            pltpu.VMEM((rows + 8, local_w), f32),
            pltpu.VMEM((rows, local_w), bf16),
            pltpu.VMEM((rows + 8, local_w), f32),
            pltpu.VMEM((4, local_w), f32),
            pltpu.VMEM((rows, 1), f32),
            pltpu.VMEM((steps, tn, local_w), bf16),
            pltpu.VMEM((steps, tn, local_w), bf16),
            pltpu.VMEM((steps, rows, tn), bf16),
            pltpu.SemaphoreType.DMA((3 + 3 * steps,)),
        ],
        cost_estimate=pl.CostEstimate(
            flops=4 * rows * local_w * width,
            bytes_accessed=4 * local_w * width + 8 * rows * width,
            transcendentals=0,
        ),
        compiler_params=pltpu.CompilerParams(vmem_limit_bytes=SMALL_VMEM),
        name="tail",
    )(odd, dconv, far, later, dy, gdecay, *in_hbm(pad, cw, r_one, xw, yw, x_low))


def join_kernel(first, last, at, reverse, flag_ref, total_ref, other_ref, *refs):
    before_ref = None if first else refs[0]
    outs = refs if first else refs[1:]
    own_a, own_b = total_ref[0:1, :], total_ref[1:2, :]
    far_a, far_b = other_ref[0:1, :], other_ref[1:2, :]
    upper = jnp.full(own_a.shape, flag_ref[at], jnp.int32)
    far_first = upper == (0 if reverse else 1)
    if first:
        new_a = jnp.where(far_first, far_a, 1.0)
        new_b = jnp.where(far_first, far_b, 0.0)
    else:
        old_a, old_b = before_ref[0:1, :], before_ref[1:2, :]
        new_a = jnp.where(far_first, far_a * old_a, old_a)
        new_b = jnp.where(far_first, old_a * far_b + old_b, old_b)
    if last:
        outs[0][...] = new_b
        return
    outs[0][0:1, :] = new_a
    outs[0][1:2, :] = new_b
    outs[1][0:1, :] = own_a * far_a
    outs[1][1:2, :] = jnp.where(far_first, own_a * far_b + own_b, far_a * own_b + far_b)


def carried(odd, total, reverse):
    size = lax.axis_size("seq")
    pair = (total.shape, jnp.float32)
    before = None
    bit, at = 1, 3
    while bit < size:
        other = swap(total, "seq", bit)
        last = 2 * bit >= size
        args = (total, other) if before is None else (total, other, before)
        outs = [((1, total.shape[1]), jnp.float32)] if last else [pair, pair]
        kernel = functools.partial(join_kernel, before is None, last, at, reverse)
        joined = small_call(kernel, outs, (odd,), *args)
        before, total = (joined[0], None) if last else joined
        bit, at = 2 * bit, at + 1
    return before


def low_kernel(keep_ref, far_ref, low_ref):
    low_ref[...] = (keep_ref[...] + far_ref[...]).astype(jnp.bfloat16)


def low_sum_kernel(low_ref, far_ref, out_ref):
    out_ref[...] = (
        low_ref[...].astype(jnp.float32) + far_ref[...].astype(jnp.float32)
    ).astype(jnp.bfloat16)


def pair_sum(keep, send):
    far = swap(send, "mp", 1)
    bf16 = [(keep.shape, jnp.bfloat16)]
    (low,) = small_call(low_kernel, bf16, (), keep, far)
    bit = 2
    while True:
        far = swap(low, "mp", bit)
        bit *= 2
        if bit >= lax.axis_size("mp"):
            return low, far
        (low,) = small_call(low_sum_kernel, bf16, (), low, far)


def total_of(low_ref, far_ref):
    return low_ref[...].astype(jnp.float32) + far_ref[...].astype(jnp.float32)


def norm_two_kernel(
    odd_ref, x_ref, low_ref, far_ref, gain_ref, mixed_ref, x_one_ref, n_ref, r_ref, own_ref, out_ref
):
    half, width = low_ref.shape
    local_w = mixed_ref.shape[1]
    x_one = x_ref[...].astype(jnp.float32) + total_of(low_ref, far_ref)
    r = lax.rsqrt(jnp.mean(x_one * x_one, axis=-1, keepdims=True) + EPS)
    n = x_one * r
    normed = (n * gain_ref[...].reshape(1, width)).astype(jnp.bfloat16)
    x_one_ref[...] = x_one
    n_ref[...] = n
    r_ref[...] = r
    own_ref[...] = normed
    out_ref[:, 0:width] = normed
    out_ref[:, width : width + local_w] = mixed_ref[0:half, :]
    out_ref[:, width + local_w :] = mixed_ref[half:, :]


def d_x_kernel(
    odd_ref, low_ref, far_ref, gain_ref, n_ref, r_ref, cot_ref, d_x_ref, d_low_ref, g_ref
):
    d_n = total_of(low_ref, far_ref)
    n = n_ref[...]
    g_ref[...] = jnp.sum(d_n * n, axis=0, keepdims=True)
    e = gain_ref[...].reshape(1, n.shape[1]) * d_n
    mean = jnp.mean(e * n, axis=-1, keepdims=True)
    d_x = cot_ref[...].astype(jnp.float32) + r_ref[...] * (e - n * mean)
    d_x_ref[...] = d_x
    d_low_ref[...] = d_x.astype(jnp.bfloat16)


def far_kernel(far_ref, later_ref, out_ref):
    rows, rest = far_ref.shape
    out_ref[0:rows, :] = far_ref[...]
    out_ref[rows:, :] = later_ref[:, later_ref.shape[1] - rest :]


def pack_kernel(
    odd_ref, normed_ref, gx_ref, ga_ref, vec_ref, mix_ref, d_x_ref, ffn_ref, out_ref
):
    blocks, _, span = out_ref.shape
    half = normed_ref.shape[0]
    cols = span // 2
    head, local_w = gx_ref.shape
    tall = head // blocks
    pieces = local_w // span
    bf16 = jnp.bfloat16

    def parts(value):
        high = value.astype(bf16)
        return high, (value - high.astype(jnp.float32)).astype(bf16)

    out_ref[:, half + 2 * tall * pieces :, :] = jnp.zeros((blocks, 8, span), bf16)
    thin = local_w // blocks
    for s in range(blocks):
        out_ref[s, 0:half, 0:cols] = normed_ref[:, s * cols : (s + 1) * cols]
        out_ref[s, 0:half, cols:] = d_x_ref[:, s * cols : (s + 1) * cols]
        for g, ref in enumerate((gx_ref, ga_ref)):
            for q in range(pieces):
                at = half + (g * pieces + q) * tall
                out_ref[s, at : at + tall, :] = ref[
                    s * tall : (s + 1) * tall, q * span : (q + 1) * span
                ].astype(bf16)
        at = half + 2 * tall * pieces
        both = jnp.concatenate(
            [ffn_ref[:, s * cols : (s + 1) * cols], mix_ref[:, s * cols : (s + 1) * cols]], axis=1
        )
        row = lax.broadcasted_iota(jnp.int32, (8, span), 0)
        high, rest = parts(both)
        lines = jnp.where(row == 6, high.astype(jnp.float32), rest.astype(jnp.float32))
        out_ref[s, at : at + 8, :] = jnp.where(row < 6, 0.0, lines).astype(bf16)
        high, rest = parts(vec_ref[0:6, s * thin : (s + 1) * thin])
        out_ref[s, at : at + 6, 0:thin] = high
        out_ref[s, at : at + 6, cols : cols + thin] = rest


def last_kernel(
    odd_ref, x_ref, r_ref, low_ref, far_ref, gain_ref, d_x_ref, out_ref
):
    d_n = total_of(low_ref, far_ref)
    r = r_ref[...]
    n = x_ref[...].astype(jnp.float32) * r
    e = gain_ref[...].reshape(1, n.shape[1]) * d_n
    mean = jnp.mean(e * n, axis=-1, keepdims=True)
    out_ref[...] = (d_x_ref[...] + r * (e - n * mean)).astype(jnp.bfloat16)


def out_own_kernel(odd_ref, low_ref, far_ref, x_one_ref, out_ref):
    out_ref[...] = (x_one_ref[...] + total_of(low_ref, far_ref)).astype(jnp.bfloat16)


def order_kernel(odd_ref, own_ref, far_ref, out_ref):
    half = own_ref.shape[0]

    def body(odd):
        out_ref[odd * half : (odd + 1) * half, :] = own_ref[...]
        out_ref[(1 - odd) * half : (2 - odd) * half, :] = far_ref[...]

    either(odd_ref, body)


def per_device(
    block_input,
    mix_gain,
    x_weight,
    y_weight,
    conv_weight,
    conv_bias,
    input_gate,
    decay_gate,
    decay_param,
    out_weight,
    ffn_gain,
    gate_weight,
    up_weight,
    down_weight,
    out_cotangent,
):
    seq_count, rows, width = block_input.shape
    local_w = x_weight.shape[1]
    head = input_gate.shape[0]
    rest = local_w % head
    blocks = lax.axis_size("seq")
    place = lax.axis_index("seq").astype(jnp.int32)
    bits = [(place >> k) & 1 for k in range(max(1, (blocks - 1).bit_length()))]
    along = lax.axis_index("mp").astype(jnp.int32)
    odd = jnp.stack([along & 1, place, along >> 1] + bits)
    share = lax.axis_size("mp") // 2
    assert share == 2
    half = rows // 2
    cols = width // blocks
    bf16, f32 = jnp.bfloat16, jnp.float32
    half_wide = (half, width)

    x_low = block_input.reshape(rows, width)
    cot_low = out_cotangent.reshape(rows, width)

    cot_own, cot_part, tail_rows = start(odd, cot_low, x_low, share)
    cot_part = lax.all_gather(cot_part, "seq", axis=0, tiled=True)
    cot_across = swap(cot_part, "mp", 2)
    cot_mine = braid(odd, cot_part, cot_across, blocks)
    cot_far = swap(cot_mine, "mp", 1)

    inp_tail = shifted(tail_rows, "seq", 1)
    (
        conv_now, low_now, gated_now, far_out, soft_now,
        normed1, r_one, padded, y_slope, slope_sig, conv_out, conv_low, y_gated, softer,
    ) = front(
        odd, x_low, inp_tail, mix_gain, x_weight, y_weight, conv_weight, conv_bias, decay_param, rest
    )

    prod, local_state, total, gate_x, gate_a, decay, mult, far, block_total = gates(
        odd, conv_now, low_now, swap(far_out, "mp", 1), input_gate, decay_gate, soft_now
    )
    mixed, keep, send, hidden, state_in = mix(
        odd, carried(odd, total, False), prod, local_state, gated_now, out_weight
    )

    low, high = pair_sum(keep, send)
    d_act_own = own_d_act(odd, cot_low, down_weight)
    x_one, n_two, r_two, normed2_own, gather_in = half_call(
        norm_two_kernel, odd, (x_low,), (low, high, ffn_gain, mixed),
        [
            (half_wide, f32), (half_wide, f32), ((half, 1), f32), (half_wide, bf16),
            ((half, width + 2 * local_w), bf16),
        ],
    )
    normed2_far_own = swap(normed2_own, "mp", 1)
    normed2_mine = lax.all_gather(gather_in, "seq", axis=0, tiled=True)
    normed2_far = swap(normed2_mine, "mp", 1)

    keep, send, act_own = ffn_own(
        normed2_own, normed2_far_own, d_act_own, gate_weight, up_weight
    )
    low, high = pair_sum(keep, send)
    out_keep, out_send = ffn_out(act_own, down_weight)
    d_x_one, d_x_low, g_ffn_gain = half_call(
        d_x_kernel, odd, (), (low, high, ffn_gain),
        [(half_wide, f32), (half_wide, bf16), ((1, width), f32)], (n_two, r_two, cot_own),
    )

    d_y_low, local_lam, after_prod, total = back(
        odd, d_x_low, swap(d_x_low, "mp", 1), out_weight, hidden, y_gated, y_slope, decay, block_total
    )
    low, high = pair_sum(out_keep, out_send)
    (out_own,) = half_call(out_own_kernel, odd, (), (low, high), [(half_wide, bf16)], (x_one,))
    out_far = swap(out_own, "mp", 1)
    returned = carried(odd, total, True)
    d_conv, d_far, halo, g_input, g_decay_gate, g_decay = gates_back(
        odd, returned, state_in, local_lam, after_prod, hidden, decay, mult, conv_out, conv_low,
        far, gate_x, gate_a, input_gate, decay_gate, softer, slope_sig,
    )
    later = shifted(halo, "seq", -1)
    (far_out,) = small_call(far_kernel, [((rows + 8, rest), f32)], (), d_far, later)
    keep, send, branch_in, vectors, g_mix_gain = tail(
        odd, d_conv, swap(far_out, "mp", 1), later, padded, conv_weight, d_y_low, g_decay,
        x_weight, y_weight, x_low, r_one,
    )
    branches = lax.all_gather(branch_in, "seq", axis=0, tiled=True)
    low, high = pair_sum(keep, send)

    span = 2 * cols
    gate_rows = 2 * head // blocks * (local_w // span)
    (packed,) = half_call(
        pack_kernel, odd, (normed1,),
        (g_input, g_decay_gate, vectors, g_mix_gain),
        [((blocks, half + gate_rows + 8, span), bf16)], (d_x_low, g_ffn_gain),
    )
    packed = lax.all_to_all(packed, "seq", split_axis=0, concat_axis=0, tiled=True)
    g_gate, g_up, g_down = ffn_all(
        odd, cols, normed2_mine, normed2_far, cot_mine, cot_far,
        gate_weight, up_weight, down_weight,
    )
    packed, g_gate = lax.optimization_barrier((packed, g_gate))
    (in_own,) = half_call(
        last_kernel, odd, (x_low, r_one), (low, high, mix_gain),
        [(half_wide, bf16)], (d_x_one,),
    )
    order = lambda own, far: small_call(order_kernel, [((rows, width), bf16)], (odd,), own, far)[0]
    input_grad = order(in_own, swap(in_own, "mp", 1))
    block_output = order(out_own, out_far)

    packed_far = swap(packed, "mp", 1)
    g_in, g_dec, small, gains = small_call(
        functools.partial(sums_kernel, cols, half),
        [
            ((head // blocks, local_w), f32), ((head // blocks, local_w), f32),
            ((8, local_w // blocks), f32), ((8, span), f32),
        ],
        (), packed,
    )
    g_out, g_y, g_x = token_grads(
        odd, normed2_mine, width // local_w, branches, packed, packed_far, half, local_w
    )
    near = gains + swap(gains, "mp", 1)
    bit = 2
    wider = near
    while bit < lax.axis_size("mp"):
        wider = wider + swap(wider, "mp", bit)
        bit *= 2

    shape = (seq_count, rows, width)
    return (
        block_output.reshape(shape),
        input_grad.reshape(shape),
        wider[0, cols:],
        g_x,
        g_y,
        small[:4],
        small[4],
        g_in,
        g_dec,
        small[5],
        g_out.T,
        near[0, :cols],
        g_gate,
        g_up,
        g_down.T,
    )


def solution(mesh):
    in_specs = (
        P(None, "seq", None),
        P(),
        P(None, "mp"),
        P(None, "mp"),
        P(None, "mp"),
        P("mp"),
        P(None, "mp"),
        P(None, "mp"),
        P("mp"),
        P("mp", None),
        P(),
        P(None, "mp"),
        P(None, "mp"),
        P("mp", None),
        P(None, "seq", None),
    )
    out_specs = (
        P(None, "seq", None),
        P(None, "seq", None),
        P("seq"),
        P("seq", "mp"),
        P("seq", "mp"),
        P(None, ("mp", "seq")),
        P(("mp", "seq")),
        P("seq", "mp"),
        P("seq", "mp"),
        P(("mp", "seq")),
        P("mp", "seq"),
        P("seq"),
        P("seq", "mp"),
        P("seq", "mp"),
        P("mp", "seq"),
    )

    return jax.shard_map(
        per_device, mesh=mesh, in_specs=in_specs, out_specs=out_specs, check_vma=False
    )
```

time: 2180 us -> 359 us (0.16)
  waiting for transfers between devices: 1600 us -> 150 us
  local copies, waits for them, and re-layouts: 193 us -> 6.06 us
  Pallas kernels: 0 us -> 154 us
  blocking collectives: 138 us -> 0 us
  other arithmetic: 115 us -> 0.67 us
  matrix products: 101 us -> 0 us
  starting transfers between devices: 7.34 us -> 32.9 us
    reduce_scatter x9 -> x0, waiting for transfers between devices: 1460 us -> none  [the longest x1 328 us: per_device(): lax.psum_scatter(g_down, 'seq', scatter_dimension=1, tiled=True)]
    pallas_call x0 -> x32, Pallas kernels: none -> 154 us  [the longest x1 58.7 us: ffn_all(): pl.pallas_call(functools.partial(ffn_all_kernel, sub, span), grid=(local_...]
    psum x3 -> x0, waiting for transfers between devices: 130 us -> none  [the longest x1 60.4 us: per_device(): ffn_out = lax.psum(bdot(act, down_weight), 'mp')]
    dot_general x24 -> x0, matrix products: 101 us -> none  [bdot(): return jnp.dot(left, right, preferred_element_type=jnp.float32)]
    all_gather x4 -> x0, blocking collectives: 100 us -> none  [the longest x3 91.7 us: carried_in(): pieces = jax.tree.map(lambda part: lax.all_gather(part, axis), value)]
    slice x102 -> x1, local copies, waits for them, and re-layouts: 88.3 us -> 0.58 us  [per_device(): small[:4]]
    all_gather x0 -> x3, waiting for transfers between devices: none -> 81.3 us  [the longest x1 81.3 us: per_device(): normed2_mine = lax.all_gather(gather_in, 'seq', axis=0, tiled=True)]
    pad x48 -> x0, local copies, waits for them, and re-layouts: 63.4 us -> none  [the longest x24 40.1 us: per_device(): lax.associative_scan(link_pairs, (decay_next, direct), reverse=True, axis=1)]
  transfers between devices with their start and end apart: 15 -> 32, of which waited for: 13 -> 20; matrix products, arithmetic and copies ran while one was open for 5% -> 0% of each run, Pallas kernels for 0% -> 40%
where the time goes in v1:
time: 359 us; the launch traced here: 358 us
  Pallas kernels  154 us (43%)
  waiting for transfers between devices  150 us (42%)
  starting transfers between devices  32.9 us (9%)
  between operations  14.3 us (4%)
  local copies, waits for them, and re-layouts  6.06 us (2%)
    all_gather x1, waiting for transfers between devices, per_device(): normed2_mine = lax.all_gather(gather_in, 'seq', axis=0, tiled=True)  81.3 us
    ppermute x26, waiting for transfers between devices, swap(): return lax.ppermute(value, axis, [(i, i ^ bit) for i in range(size)])  59.1 us
    pallas_call x1, Pallas kernels, ffn_all(): pl.pallas_call(functools.partial(ffn_all_kernel, sub, span), grid=(local_...  58.7 us
    ppermute x26, starting transfers between devices, swap(): return lax.ppermute(value, axis, [(i, i ^ bit) for i in range(size)])  22.6 us
    pallas_call x5, Pallas kernels, half_call(): pl.pallas_call(kernel, grid_spec=pltpu.PrefetchScalarGridSpec(num_scalar_...  15.5 us
    pallas_call x1, Pallas kernels, ffn_own(): pl.pallas_call(ffn_own_kernel, in_specs=[vmem] * 2 + [hbm] * 3, out_specs...  12.8 us
    pallas_call x14, Pallas kernels, small_call(): pl.pallas_call(kernel, in_specs=scalars + [vmem] * len(args), out_specs=[...  8.54 us
    pallas_call x1, Pallas kernels, tail(): pl.pallas_call(tail_kernel, in_specs=[pl.BlockSpec(memory_space=pltpu.SME...  8.02 us
  transfers between devices with their start and end apart: 32, of which 20 were waited for; matrix products, arithmetic and copies ran while one was open for 0% of the time, Pallas kernels for 40%

profile of v1, /device:TPU:0, one launch (start us, length us, event | category | flops | bytes accessed | tf_op | source)
XLA Modules:
  0.0 358.2 jit_solution(3487652763029515243)
XLA Ops:
  7.3 2.4 start.1
  9.9 5.0 %collective-permute-start = (bf16[8,2560]{1,0:T(8,128)(2,1)S(1)}, bf16[8,2560]{1,0:T(8,128)(2,1)S(1)}, u32[]{:S(2)}, u32[]{:S(2)}) collective-permute-start(bf16[8,2560]{1,0:T(8,128)(2,1)S(1)} %get-tuple-element.94), channel_id=1, source_target_pairs={{0,4},{4,8},{8,12},{12,16},{16,20},{20,24},{24,28},{1,5},{5,9},{9,... | collective-permute-start | bytes 122888 | tf_op jit(solution)/shard_map/ppermute | solution.py:49
  14.9 1.7 collective-permute-done.tail_ref
  16.6 6.0 %front.1 = (f32[160,640]{1,0:T(8,128)S(1)}, bf16[160,640]{1,0:T(8,128)(2,1)S(1)}, f32[160,640]{1,0:T(8,128)S(1)}, bf16[160,128]{1,0:T(8,128)(2,1)S(1)}, f32[1,64...) custom-call(s32[6]{0:T(128)S(1)} %stack.27.odd_ref.flag_ref.place_re, ...), custom_call_target="tpu_custom_call" | custom-call | flops 1048576000 | bytes 8192000 | tf_op jit(solution)/shard_map/front/pallas_call | solution.py:230
  23.9 2.7 gates.1
  26.6 2.4 collective-permute-start.2
  29.0 1.6 collective-permute-done.2.other_ref
  31.1 3.1 collective-permute-start.3
  34.2 1.6 collective-permute-done.3.other_ref
  36.4 3.1 collective-permute-start.4
  39.5 1.6 collective-permute-done.4.other_ref
  41.7 4.2 %mix.1 = (bf16[160,640]{1,0:T(8,128)(2,1)S(1)}, f32[80,2560]{1,0:T(8,128)S(1)}, f32[80,2560]{1,0:T(8,128)S(1)}, f32[160,640]{1,0:T(8,128)}, f32[1,640]{1,0:T(1,128)}) custom-call(s32[6]{0:T(128)S(1)} %stack.27.odd_ref.flag_ref.place_ref, f32[1,640]{1,0:T(1,128)S(1)} %shard_map.264.state_in_ref, f32[160,640]{1,0:T(8,128)S(1)} %get-tuple-element.104.prod_ref, ...), custom_call_target="tpu_custom_call" | custom-call | flops 524288000 | bytes 4915200 | tf_op jit(solution)/shard_map/mix/pallas_call | solution.py:431
  46.0 2.3 collective-permute-done.5.far_ref
  48.4 1.6 collective-permute-start.6
  49.9 10.0 %collective-permute-done.6.far_ref = bf16[80,2560]{1,0:T(8,128)(2,1)S(1)} collective-permute-done((bf16[80,2560]{1,0:T(8,128)(2,1)S(1)}, bf16[80,2560]{1,0:T(8,128)(2,1)S(1)}, u32[]{:S(2)}, u32[]{:S(2)}) %collective-permute-start.6) | collective-permute-done | bytes 409632 | tf_op jit(solution)/shard_map/ppermute | solution.py:44
  59.9 3.4 shard_map.266
  63.4 1.6 collective-permute-start.23
  65.0 81.3 %all-gather.4.cloned.1.call-done.n_ref.mixed_ref.mfar_ref = bf16[640,3840]{1,0:T(8,128)(2,1)} async-done(((bf16[80,3840]{1,0:T(8,128)(2,1)}), bf16[640,3840]{1,0:T(8,128)(2,1)}) %all-gather.4.cloned.1.call-update) | async-done | bytes 4915216 | tf_op jit(solution)/shard_map/all_gather | solution.py:1321
  147.5 6.9 %braid.1.c_ref = bf16[640,2560]{1,0:T(8,128)(2,1)} custom-call(s32[6]{0:T(128)S(1)} %stack.27.odd_ref.flag_ref.place_ref, bf16[320,2560]{1,0:T(8,128)(2,1)} %all-gather.6.cloned.1.call-done.own_ref, bf16[320,2560]{1,0:T(8,128)(2,1)} %copy-done.28), custom_call_target="tpu_custom_call" | custom-call | bytes 6553600 | tf_op jit(solution)/shard_map/braid/pallas_call | solution.py:526
  155.0 6.5 %own_d_act.1.da_ref = f32[160,1920]{1,0:T(8,128)S(1)} custom-call(s32[6]{0:T(128)S(1)} %stack.27.odd_ref.flag_ref.place_ref, bf16[160,2560]{1,0:T(8,128)(2,1)} %bitcast.23, bf16[1920,2560]{1,0:T(8,128)(2,1)} %dw_ref.5), custom_call_target="tpu_custom_call" | custom-call | flops 1572864000 | bytes 9830400 | tf_op jit(solution)/shard_map/own_d_act/pallas_call | solution.py:560
  161.5 12.8 %ffn_own.1 = (f32[80,2560]{1,0:T(8,128)S(1)}, f32[80,2560]{1,0:T(8,128)S(1)}, bf16[160,1920]{1,0:T(8,128)(2,1)S(1)}) custom-call(bf16[80,2560]{1,0:T(8,128)(2,1)S(1)} %collective-permute-done.7.nfar_ref, f32[160,1920]{1,0:T(8,128)S(1)} %own_d_act.1.da_ref, bf16[80,2560]{1,0:T(8,128)(2,1)} %get-tuple-element.110.n_hbm, bf16[2560,1920]{1,0:T(8,128)(2,1)} %gw_ref.1, ...), custom_call_target="tpu_custom_call" | custom-call | flops 6291456000 | bytes 19660800 | tf_op jit(solution)/shard_map/ffn_own/pallas_call | solution.py:624
  174.9 2.0 collective-permute-done.11.far_ref
  177.1 1.5 collective-permute-start.12
  178.6 10.3 %collective-permute-done.12.far_ref = bf16[80,2560]{1,0:T(8,128)(2,1)S(1)} collective-permute-done((bf16[80,2560]{1,0:T(8,128)(2,1)S(1)}, bf16[80,2560]{1,0:T(8,128)(2,1)S(1)}, u32[]{:S(2)}, u32[]{:S(2)}) %collective-permute-start.12) | collective-permute-done | bytes 409632 | tf_op jit(solution)/shard_map/ppermute | solution.py:44
  188.9 3.4 shard_map.271
  192.3 1.9 collective-permute-done.13.far_ref
  195.3 5.4 %back.1 = (bf16[160,640]{1,0:T(8,128)(2,1)S(1)}, f32[160,640]{1,0:T(8,128)S(1)}, f32[160,640]{1,0:T(8,128)S(1)}, f32[2,640]{1,0:T(2,128)S(1)}) custom-call(s32[6]{0:T(128)S(1)} %stack.27.odd_ref.flag_ref.place_ref, bf16[80,2560]{1,0:T(8,128)(2,1)S(1)} %copy-done.1, bf16[80,2560]{1,0:T(8,128)(2,1)S(1)} %collective-permute-done.13.far_ref, ...), custom_call_target="tpu_custom_call" | custom-call | flops 524288000 | bytes 6348800 | tf_op jit(solution)/shard_map/back/pallas_call | solution.py:887
  201.4 3.1 collective-permute-done.14.other_ref
  205.9 2.8 collective-permute-done.15.other_ref
  209.2 1.7 collective-permute-start.16
  210.9 2.9 collective-permute-done.16.other_ref
  214.4 1.7 gates_back.1
  217.4 4.4 %collective-permute-done.17.later_ref = f32[8,768]{1,0:T(8,128)S(1)} collective-permute-done((f32[8,768]{1,0:T(8,128)S(1)}, f32[8,768]{1,0:T(8,128)S(1)}, u32[]{:S(2)}, u32[]{:S(2)}) %collective-permute-start.17) | collective-permute-done | bytes 24608 | tf_op jit(solution)/shard_map/ppermute | solution.py:49
  223.2 8.0 %tail.1 = (f32[80,2560]{1,0:T(8,128)S(1)}, f32[80,2560]{1,0:T(8,128)}, bf16[80,2560]{1,0:T(8,128)(2,1)}, f32[8,640]{1,0:T(8,128)S(1)}, f32[1,2560]{1,0:T(1,128)S(1)}) custom-call(s32[6]{0:T(128)S(1)} %stack.27.odd_ref.flag_ref.place_ref, f32[160,640]{1,0:T(8,128)S(1)} %get-tuple-element.143.dconv_ref, f32[168,128]{1,0:T(8,128)S(1)} %collective-permute-done.18.far_ref, ...), custom_call_target="tpu_custom_call" | custom-call | flops 1048576000 | bytes 9830400 | tf_op jit(solution)/shard_map/tail/pallas_call | solution.py:1055
  231.3 7.2 %ffn_out.1 = (f32[80,2560]{1,0:T(8,128)S(1)}, f32[80,2560]{1,0:T(8,128)}) custom-call(bf16[160,1920]{1,0:T(8,128)(2,1)S(1)} %get-tuple-element.111.act_ref, bf16[1920,2560]{1,0:T(8,128)(2,1)} %dw_ref.5), custom_call_target="tpu_custom_call" | custom-call | flops 1572864000 | bytes 9830400 | tf_op jit(solution)/shard_map/ffn_out/pallas_call | solution.py:660
  239.9 3.2 shard_map.279
  243.1 3.8 %all-to-all-start = ((bf16[8,152,640]{2,1,0:T(8,128)(2,1)}), bf16[8,152,640]{2,1,0:T(8,128)(2,1)S(1)}, u32[]{:S(2)}, u32[]{:S(2)}) async-start(bf16[8,152,640]{2,1,0:T(8,128)(2,1)} %shard_map.279), calls=%async_computation | async-start | bytes 3112960 | tf_op jit(solution)/shard_map/all_to_all | solution.py:1361
  246.9 58.7 %ffn_all.1 = (f32[320,1920]{1,0:T(8,128)}, f32[320,1920]{1,0:T(8,128)}, f32[320,1920]{1,0:T(8,128)}) custom-call(s32[6]{0:T(128)} %copy-done.18, bf16[640,3840]{1,0:T(8,128)(2,1)} %all-gather.4.cloned.1.call-done.n_ref.mixed_ref.mfar_ref, bf16[640,3840]{1,0:T(8,128)(2,1)} %collective-permute-done.22.nfar_ref, bf16[640,2560]{1,0:T(8,128)(2,1)} %braid.1.c_ref, ...), custom_call_target="tpu_custom_call" | custom-call | flops 42467328000 | bytes 49971200 | tf_op jit(solution)/shard_map/ffn_all/pallas_call | solution.py:741
  305.6 3.5 all-to-all-done.packed_ref.own_ref
  309.1 1.7 copy-done.9
  312.1 1.6 collective-permute-start.9
  314.3 10.2 %collective-permute-done.9.far_ref = bf16[80,2560]{1,0:T(8,128)(2,1)S(1)} collective-permute-done((bf16[80,2560]{1,0:T(8,128)(2,1)S(1)}, bf16[80,2560]{1,0:T(8,128)(2,1)S(1)}, u32[]{:S(2)}, u32[]{:S(2)}) %collective-permute-start.9) | collective-permute-done | bytes 409632 | tf_op jit(solution)/shard_map/ppermute | solution.py:44
  324.5 2.6 shard_map.268.own_ref
  327.0 5.2 %collective-permute-done.20.far_ref = bf16[80,2560]{1,0:T(8,128)(2,1)S(1)} collective-permute-done((bf16[80,2560]{1,0:T(8,128)(2,1)S(1)}, bf16[80,2560]{1,0:T(8,128)(2,1)S(1)}, u32[]{:S(2)}, u32[]{:S(2)}) %collective-permute-start.20) | collective-permute-done | bytes 409632 | tf_op jit(solution)/shard_map/ppermute | solution.py:44
  332.2 3.1 shard_map.277.own_ref
  336.6 1.5 shard_map.269
  339.6 1.6 collective-permute-start.26
  344.1 7.5 %token_grads.1 = (f32[320,640]{1,0:T(8,128)}, f32[320,640]{1,0:T(8,128)}, f32[320,640]{1,0:T(8,128)}) custom-call(s32[6]{0:T(128)} %copy-done.18, bf16[640,3840]{1,0:T(8,128)(2,1)} %all-gather.4.cloned.1.call-done.n_ref.mixed_ref.mfar_ref, bf16[640,3840]{1,0:T(8,128)(2,1)} %all-gather.4.cloned.1.call-done.n_ref.mixed_ref.mfar_ref, ...), custom_call_target="tpu_custom_call" | custom-call | flops 1572864000 | bytes 6553600 | tf_op jit(solution)/shard_map/token_grads/pallas_call | solution.py:810
  (116 shorter events, 21.7 us)
Async XLA Ops:
  7.2 56.2 %all-gather.6.cloned.1.call-start = ((), (), s32[]{:S(2)}) async-start(), calls=%async_computation.2 | async-start | bytes 1843200 | tf_op jit(solution)/shard_map/all_gather | solution.py:1291
  7.3 232.6 %copy-start.18 = (s32[6]{0:T(128)}, s32[6]{0:T(128)S(1)}, u32[]{:S(2)}) copy-start(s32[6]{0:T(128)S(1)} %stack.27.odd_ref.flag_ref.place_ref) | copy-start | bytes 76
  9.8 136.5 %all-gather.4.cloned.1.call-start = ((), (), s32[]{:S(2)}) async-start(), calls=%async_computation.1 | async-start | bytes 5529600 | tf_op jit(solution)/shard_map/all_gather | solution.py:1321
  9.9 6.7 %collective-permute-start = (bf16[8,2560]{1,0:T(8,128)(2,1)S(1)}, bf16[8,2560]{1,0:T(8,128)(2,1)S(1)}, u32[]{:S(2)}, u32[]{:S(2)}) collective-permute-start(bf16[8,2560]{1,0:T(8,128)(2,1)S(1)} %get-tuple-element.94), channel_id=1, source_target_pairs={{0,4},{4,8},{8,12},{12,16},{16,20},{20,24},{24,28},{1,5},{5,9},{9,... | collective-permute-start | bytes 122888 | tf_op jit(solution)/shard_map/ppermute | solution.py:49
  22.6 1.3 collective-permute-start.1
  26.6 4.0 %collective-permute-start.2 = (f32[2,640]{1,0:T(2,128)S(1)}, f32[2,640]{1,0:T(2,128)S(1)}, u32[]{:S(2)}, u32[]{:S(2)}) collective-permute-start(f32[2,640]{1,0:T(2,128)S(1)} %get-tuple-element.99.total_ref), channel_id=1, source_target_pairs={{0,4},{4,0},{8,12},{12,8},{16,20},{20,16},{24,28},{28,24},{1,5},{5... | collective-permute-start | bytes 15368 | tf_op jit(solution)/shard_map/ppermute | solution.py:44
  31.1 4.7 %collective-permute-start.3 = (f32[2,640]{1,0:T(2,128)S(1)}, f32[2,640]{1,0:T(2,128)S(1)}, u32[]{:S(2)}, u32[]{:S(2)}) collective-permute-start(f32[2,640]{1,0:T(2,128)S(1)} %get-tuple-element.100.total_ref), channel_id=1, source_target_pairs={{0,8},{4,12},{8,0},{12,4},{16,24},{20,28},{24,16},{28,20},{1,9},{5... | collective-permute-start | bytes 15368 | tf_op jit(solution)/shard_map/ppermute | solution.py:44
  36.4 4.7 %collective-permute-start.4 = (f32[2,640]{1,0:T(2,128)S(1)}, f32[2,640]{1,0:T(2,128)S(1)}, u32[]{:S(2)}, u32[]{:S(2)}) collective-permute-start(f32[2,640]{1,0:T(2,128)S(1)} %get-tuple-element.102.total_ref), channel_id=1, source_target_pairs={{0,16},{4,20},{8,24},{12,28},{16,0},{20,4},{24,8},{28,12},{1,17},{... | collective-permute-start | bytes 15368 | tf_op jit(solution)/shard_map/ppermute | solution.py:44
  45.9 2.4 collective-permute-start.5
  48.4 11.6 %collective-permute-start.6 = (bf16[80,2560]{1,0:T(8,128)(2,1)S(1)}, bf16[80,2560]{1,0:T(8,128)(2,1)S(1)}, u32[]{:S(2)}, u32[]{:S(2)}) collective-permute-start(bf16[80,2560]{1,0:T(8,128)(2,1)S(1)} %shard_map.265.low_ref), channel_id=1, source_target_pairs={{0,2},{1,3},{2,0},{3,1},{4,6},{5,7},{6,4},{7,5},{8,10},{9,11},{10,... | collective-permute-start | bytes 1228808 | tf_op jit(solution)/shard_map/ppermute | solution.py:44
  63.3 91.6 %copy-start.29 = (bf16[80,2560]{1,0:T(8,128)(2,1)S(1)}, bf16[80,2560]{1,0:T(8,128)(2,1)}, u32[]{:S(2)}) copy-start(bf16[80,2560]{1,0:T(8,128)(2,1)} %get-tuple-element.110.n_hbm) | copy-start | bytes 1228804
  63.3 280.8 %all-gather.8.cloned.1.call-start = ((), (), s32[]{:S(2)}) async-start(), calls=%async_computation.3 | async-start | bytes 3686400 | tf_op jit(solution)/shard_map/all_gather | solution.py:1351
  63.4 82.9 %collective-permute-start.23 = (bf16[320,2560]{1,0:T(8,128)(2,1)}, bf16[320,2560]{1,0:T(8,128)(2,1)S(1)}, u32[]{:S(2)}, u32[]{:S(2)}) collective-permute-start(bf16[320,2560]{1,0:T(8,128)(2,1)} %all-gather.6.cloned.1.call-done.own_ref), channel_id=1, source_target_pairs={{0,2},{1,3},{2,0},{3,1},{4,6},{5,7},{6,4},{7,5},{8,10},{9,11},{10,... | collective-permute-start | bytes 4915208 | tf_op jit(solution)/shard_map/ppermute | solution.py:44
  146.3 100.6 %collective-permute-start.22 = (bf16[640,3840]{1,0:T(8,128)(2,1)}, bf16[640,3840]{1,0:T(8,128)(2,1)}, u32[]{:S(2)}, u32[]{:S(2)}) collective-permute-start(bf16[640,3840]{1,0:T(8,128)(2,1)} %all-gather.4.cloned.1.call-done.n_ref.mixed_ref.mfar_ref), channel_id=1, source_target_pairs={{0,1},{1,0},{2,3},{3,2},{4,5},{5,4},{6,7},{7,6},{8,9},{9,8},{10,11... | collective-permute-start | bytes 14745608 | tf_op jit(solution)/shard_map/ppermute | solution.py:44
  154.4 92.5 %collective-permute-start.24 = (bf16[640,2560]{1,0:T(8,128)(2,1)}, bf16[640,2560]{1,0:T(8,128)(2,1)}, u32[]{:S(2)}, u32[]{:S(2)}) collective-permute-start(bf16[640,2560]{1,0:T(8,128)(2,1)} %braid.1.c_ref), channel_id=1, source_target_pairs={{0,1},{1,0},{2,3},{3,2},{4,5},{5,4},{6,7},{7,6},{8,9},{9,8},{10,11... | collective-permute-start | bytes 9830408 | tf_op jit(solution)/shard_map/ppermute | solution.py:44
  154.9 6.6 %collective-permute-start.7 = (bf16[80,2560]{1,0:T(8,128)(2,1)S(1)}, bf16[80,2560]{1,0:T(8,128)(2,1)S(1)}, u32[]{:S(2)}, u32[]{:S(2)}) collective-permute-start(bf16[80,2560]{1,0:T(8,128)(2,1)S(1)} %copy-done.29), channel_id=1, source_target_pairs={{0,1},{1,0},{2,3},{3,2},{4,5},{5,4},{6,7},{7,6},{8,9},{9,8},{10,11... | collective-permute-start | bytes 1228808 | tf_op jit(solution)/shard_map/ppermute | solution.py:44
  174.4 19.9 %copy-start.4 = (f32[160,640]{1,0:T(8,128)S(1)}, f32[160,640]{1,0:T(8,128)}, u32[]{:S(2)}) copy-start(f32[160,640]{1,0:T(8,128)} %get-tuple-element.125.decay_ref) | copy-start | bytes 1228804
  174.4 19.9 %copy-start.5 = (f32[160,640]{1,0:T(8,128)S(1)}, f32[160,640]{1,0:T(8,128)}, u32[]{:S(2)}) copy-start(f32[160,640]{1,0:T(8,128)} %get-tuple-element.122.hidden_ref) | copy-start | bytes 1228804
  174.4 19.9 %copy-start.12 = (f32[160,640]{1,0:T(8,128)S(1)}, f32[160,640]{1,0:T(8,128)}, u32[]{:S(2)}) copy-start(f32[160,640]{1,0:T(8,128)} %get-tuple-element.124.slope_ref) | copy-start | bytes 1228804
  174.4 2.5 collective-permute-start.11
  177.1 11.8 %collective-permute-start.12 = (bf16[80,2560]{1,0:T(8,128)(2,1)S(1)}, bf16[80,2560]{1,0:T(8,128)(2,1)S(1)}, u32[]{:S(2)}, u32[]{:S(2)}) collective-permute-start(bf16[80,2560]{1,0:T(8,128)(2,1)S(1)} %shard_map.270.low_ref), channel_id=1, source_target_pairs={{0,2},{1,3},{2,0},{3,1},{4,6},{5,7},{6,4},{7,5},{8,10},{9,11},{10,... | collective-permute-start | bytes 1228808 | tf_op jit(solution)/shard_map/ppermute | solution.py:44
  188.9 25.5 %copy-start.14 = (f32[160,640]{1,0:T(8,128)S(1)}, f32[160,640]{1,0:T(8,128)}, u32[]{:S(2)}) copy-start(f32[160,640]{1,0:T(8,128)} %get-tuple-element.136.conv_ref) | copy-start | bytes 1228804
  188.9 25.5 %copy-start.15 = (f32[160,640]{1,0:T(8,128)S(1)}, f32[160,640]{1,0:T(8,128)}, u32[]{:S(2)}) copy-start(f32[160,640]{1,0:T(8,128)} %get-tuple-element.139.gx_ref) | copy-start | bytes 1228804
  188.9 25.5 %copy-start.16 = (f32[160,640]{1,0:T(8,128)S(1)}, f32[160,640]{1,0:T(8,128)}, u32[]{:S(2)}) copy-start(f32[160,640]{1,0:T(8,128)} %get-tuple-element.140.ga_ref) | copy-start | bytes 1228804
  188.9 25.5 %copy-start.17 = (f32[160,640]{1,0:T(8,128)S(1)}, f32[160,640]{1,0:T(8,128)}, u32[]{:S(2)}) copy-start(f32[160,640]{1,0:T(8,128)} %get-tuple-element.135.mult_ref) | copy-start | bytes 1228804
  188.9 25.5 %copy-start.20 = (bf16[160,640]{1,0:T(8,128)(2,1)S(1)}, bf16[160,640]{1,0:T(8,128)(2,1)}, u32[]{:S(2)}) copy-start(bf16[160,640]{1,0:T(8,128)(2,1)} %get-tuple-element.137.low_ref) | copy-start | bytes 614404
  188.9 25.5 %copy-start.23 = (bf16[160,128]{1,0:T(8,128)(2,1)S(1)}, bf16[160,128]{1,0:T(8,128)(2,1)}, u32[]{:S(2)}) copy-start(bf16[160,128]{1,0:T(8,128)(2,1)} %get-tuple-element.138.far_ref) | copy-start | bytes 122884
  192.2 22.2 %copy-start.25 = (f32[1,640]{1,0:T(1,128)S(1)}, f32[1,640]{1,0:T(1,128)}, u32[]{:S(2)}) copy-start(f32[1,640]{1,0:T(1,128)} %get-tuple-element.142.sig_ref) | copy-start | bytes 7684
  192.3 22.2 %copy-start.26 = (f32[1,640]{1,0:T(1,128)S(1)}, f32[1,640]{1,0:T(1,128)}, u32[]{:S(2)}) copy-start(f32[1,640]{1,0:T(1,128)} %get-tuple-element.141.soft_ref) | copy-start | bytes 7684
  192.3 22.2 %copy-start.27 = (f32[1,640]{1,0:T(1,128)S(1)}, f32[1,640]{1,0:T(1,128)}, u32[]{:S(2)}) copy-start(f32[1,640]{1,0:T(1,128)} %get-tuple-element.132.state_in_ref) | copy-start | bytes 7684
  192.3 2.0 collective-permute-start.13
  200.7 3.7 %collective-permute-start.14 = (f32[2,640]{1,0:T(2,128)S(1)}, f32[2,640]{1,0:T(2,128)S(1)}, u32[]{:S(2)}, u32[]{:S(2)}) collective-permute-start(f32[2,640]{1,0:T(2,128)S(1)} %get-tuple-element.127.total_ref), channel_id=1, source_target_pairs={{0,4},{4,0},{8,12},{12,8},{16,20},{20,16},{24,28},{28,24},{1,5},{5... | collective-permute-start | bytes 15368 | tf_op jit(solution)/shard_map/ppermute | solution.py:44
  205.0 3.7 %collective-permute-start.15 = (f32[2,640]{1,0:T(2,128)S(1)}, f32[2,640]{1,0:T(2,128)S(1)}, u32[]{:S(2)}, u32[]{:S(2)}) collective-permute-start(f32[2,640]{1,0:T(2,128)S(1)} %get-tuple-element.128.total_ref), channel_id=1, source_target_pairs={{0,8},{4,12},{8,0},{12,4},{16,24},{20,28},{24,16},{28,20},{1,9},{5... | collective-permute-start | bytes 15368 | tf_op jit(solution)/shard_map/ppermute | solution.py:44
  209.2 4.6 %collective-permute-start.16 = (f32[2,640]{1,0:T(2,128)S(1)}, f32[2,640]{1,0:T(2,128)S(1)}, u32[]{:S(2)}, u32[]{:S(2)}) collective-permute-start(f32[2,640]{1,0:T(2,128)S(1)} %get-tuple-element.130.total_ref), channel_id=1, source_target_pairs={{0,16},{4,20},{8,24},{12,28},{16,0},{20,4},{24,8},{28,12},{1,17},{... | collective-permute-start | bytes 15368 | tf_op jit(solution)/shard_map/ppermute | solution.py:44
  216.1 5.7 %collective-permute-start.17 = (f32[8,768]{1,0:T(8,128)S(1)}, f32[8,768]{1,0:T(8,128)S(1)}, u32[]{:S(2)}, u32[]{:S(2)}) collective-permute-start(f32[8,768]{1,0:T(8,128)S(1)} %get-tuple-element.145), channel_id=1, source_target_pairs={{4,0},{8,4},{12,8},{16,12},{20,16},{24,20},{28,24},{5,1},{9,5},{13... | collective-permute-start | bytes 73736 | tf_op jit(solution)/shard_map/ppermute | solution.py:49
  221.9 1.3 collective-permute-start.18
  239.4 69.8 %collective-permute-start.8 = (f32[80,2560]{1,0:T(8,128)}, f32[80,2560]{1,0:T(8,128)}, u32[]{:S(2)}, u32[]{:S(2)}) collective-permute-start(f32[80,2560]{1,0:T(8,128)} %get-tuple-element.113), channel_id=1, source_target_pairs={{0,1},{1,0},{2,3},{3,2},{4,5},{5,4},{6,7},{7,6},{8,9},{9,8},{10,11... | collective-permute-start | bytes 2457608 | tf_op jit(solution)/shard_map/ppermute | solution.py:44
  239.6 74.1 %collective-permute-start.19 = (f32[80,2560]{1,0:T(8,128)}, f32[80,2560]{1,0:T(8,128)S(1)}, u32[]{:S(2)}, u32[]{:S(2)}) collective-permute-start(f32[80,2560]{1,0:T(8,128)} %get-tuple-element.150), channel_id=1, source_target_pairs={{0,1},{1,0},{2,3},{3,2},{4,5},{5,4},{6,7},{7,6},{8,9},{9,8},{10,11... | collective-permute-start | bytes 2457608 | tf_op jit(solution)/shard_map/ppermute | solution.py:44
  243.1 66.1 %all-to-all-start = ((bf16[8,152,640]{2,1,0:T(8,128)(2,1)}), bf16[8,152,640]{2,1,0:T(8,128)(2,1)S(1)}, u32[]{:S(2)}, u32[]{:S(2)}) async-start(bf16[8,152,640]{2,1,0:T(8,128)(2,1)} %shard_map.279), calls=%async_computation | async-start | bytes 3112960 | tf_op jit(solution)/shard_map/all_to_all | solution.py:1361
  246.9 85.3 %copy-start.22 = (f32[2560]{0:T(1024)S(1)}, f32[2560]{0:T(1024)}, u32[]{:S(2)}) copy-start(f32[2560]{0:T(1024)} %gain_ref.5) | copy-start | bytes 30724
  309.1 26.2 %copy-start = (bf16[8,152,640]{2,1,0:T(8,128)(2,1)}, bf16[8,152,640]{2,1,0:T(8,128)(2,1)S(1)}, u32[]{:S(2)}) copy-start(bf16[8,152,640]{2,1,0:T(8,128)(2,1)S(1)} %all-to-all-done.packed_ref.own_ref) | copy-start | bytes 4669444
  309.1 35.0 %collective-permute-start.27 = (bf16[8,152,640]{2,1,0:T(8,128)(2,1)S(1)}, bf16[8,152,640]{2,1,0:T(8,128)(2,1)}, u32[]{:S(2)}, u32[]{:S(2)}) collective-permute-start(bf16[8,152,640]{2,1,0:T(8,128)(2,1)S(1)} %all-to-all-done.packed_ref.own_ref), channel_id=1, source_target_pairs={{0,1},{1,0},{2,3},{3,2},{4,5},{5,4},{6,7},{7,6},{8,9},{9,8},{10,11... | collective-permute-start | bytes 4669448 | tf_op jit(solution)/shard_map/ppermute | solution.py:44
  312.1 12.4 %collective-permute-start.9 = (bf16[80,2560]{1,0:T(8,128)(2,1)S(1)}, bf16[80,2560]{1,0:T(8,128)(2,1)S(1)}, u32[]{:S(2)}, u32[]{:S(2)}) collective-permute-start(bf16[80,2560]{1,0:T(8,128)(2,1)S(1)} %shard_map.267.low_ref), channel_id=1, source_target_pairs={{0,2},{1,3},{2,0},{3,1},{4,6},{5,7},{6,4},{7,5},{8,10},{9,11},{10,... | collective-permute-start | bytes 1228808 | tf_op jit(solution)/shard_map/ppermute | solution.py:44
  313.7 18.5 %collective-permute-start.20 = (bf16[80,2560]{1,0:T(8,128)(2,1)S(1)}, bf16[80,2560]{1,0:T(8,128)(2,1)S(1)}, u32[]{:S(2)}, u32[]{:S(2)}) collective-permute-start(bf16[80,2560]{1,0:T(8,128)(2,1)S(1)} %shard_map.276.low_ref), channel_id=1, source_target_pairs={{0,2},{1,3},{2,0},{3,1},{4,6},{5,7},{6,4},{7,5},{8,10},{9,11},{10,... | collective-permute-start | bytes 1228808 | tf_op jit(solution)/shard_map/ppermute | solution.py:44
  327.0 9.5 %collective-permute-start.10 = (bf16[80,2560]{1,0:T(8,128)(2,1)}, bf16[80,2560]{1,0:T(8,128)(2,1)S(1)}, u32[]{:S(2)}, u32[]{:S(2)}) collective-permute-start(bf16[80,2560]{1,0:T(8,128)(2,1)} %shard_map.268.own_ref), channel_id=1, source_target_pairs={{0,1},{1,0},{2,3},{3,2},{4,5},{5,4},{6,7},{7,6},{8,9},{9,8},{10,11... | collective-permute-start | bytes 1228808 | tf_op jit(solution)/shard_map/ppermute | solution.py:44
  335.3 2.8 collective-permute-start.21
  336.1 3.5 collective-permute-start.25
  339.6 3.8 %collective-permute-start.26 = (f32[8,640]{1,0:T(8,128)S(1)}, f32[8,640]{1,0:T(8,128)S(1)}, u32[]{:S(2)}, u32[]{:S(2)}) collective-permute-start(f32[8,640]{1,0:T(8,128)S(1)} %add.6), channel_id=1, source_target_pairs={{0,2},{1,3},{2,0},{3,1},{4,6},{5,7},{6,4},{7,5},{8,10},{9,11},{10,... | collective-permute-start | bytes 61448 | tf_op jit(solution)/shard_map/ppermute | solution.py:44
  (14 other events, 145.9 us)
Sparse Core Ops, SparseCore 0:
  10.7 47.5 all-gather.5
  63.4 82.8 all-gather.3
  231.4 84.6 all-gather.7
